TPU v7x, 128 devices: a whole 4x4x4 slice. The times are simulated.
128 devices in a mesh: probe: 4 (over x), tx: 8 (over z, core), ty: 4 (over y).
Axes of the slice: x: 4, y: 4, z: 4, core: 2. Of those that a mesh axis runs over, the one named last changes fastest.
Arguments:
- probes: float32 [16, 256, 128, 128], P('probe', 'tx', 'ty'), may hold values from -8 to 8
- coupling: float32 [7, 256, 128, 128], P(None, 'tx', 'ty'), may hold values from 0.05 to 0.35, as said below
- sensor_cell: int32 [4096], replicated, may hold values from 0 to 4194302, as said below
- sensor_frac: float32 [4096], replicated, may hold values from 0 to 1
- noise_var: float32 [4096], replicated, may hold values from 0.25 to 1
- owner_slot: int32 [4096], replicated, may hold values from 0 to 4095, each once
Outputs:
- gradient: float32 [4096], P(('probe', 'tx', 'ty'))
Inputs may be any that keep to these rules, and one draw needn't show every extreme that they name: `sensor_cell`: each entry is the flat index (x * 128 + y) * 128 + z of a grid cell with z below 127; sensors are spread unevenly over the grid. `owner_slot`: a permutation of 0 to 4095. coupling[0] lies in 0.15 to 0.35, coupling[1] and coupling[2] in 0.16 to 0.34, the others in 0.05 to 0.115.
All inputs are finite; a program needn't handle non-finite values.
Results may differ from a plain program's by a relative error of at most 0.00023.
Values sent between devices are 32-bit elements; how exact they have to be, the bound alone decides.
A program may use at most 64 MiB of HBM per device.

v0:
```python
import jax
import jax.numpy as jnp
from jax import lax
from jax.sharding import PartitionSpec as P

STEPS = 16


def padded_2(block, sides, width):
    for axis, dim in sides:
        count = lax.axis_size(axis)
        forward = [(i, i + 1) for i in range(count - 1)]
        backward = [(target, source) for source, target in forward]
        low = lax.ppermute(
            lax.slice_in_dim(block, block.shape[dim] - width, None, axis=dim), axis, forward
        )
        high = lax.ppermute(lax.slice_in_dim(block, 0, width, axis=dim), axis, backward)
        block = jnp.concatenate([low, block, high], axis=dim)
    return block


def shift_table(depth_cells):
    rows = jnp.arange(depth_cells, dtype=jnp.int32)[:, None]
    cols = jnp.arange(depth_cells, dtype=jnp.int32)[None, :]
    upper = (rows == cols + 1).astype(jnp.float32)
    lower = (rows == cols - 1).astype(jnp.float32)
    return jnp.concatenate([upper, lower], axis=1)


def advance(padded, weights_now, table):
    depth_cells = padded.shape[3]
    centre_cells = padded[:, 1:-1, 1:-1]
    vertical = jnp.einsum(
        "pxyz,zw->pxyw",
        centre_cells,
        table,
        precision=lax.Precision.HIGHEST,
        preferred_element_type=jnp.float32,
    )
    result = weights_now[0] * centre_cells
    result = result + weights_now[1] * padded[:, 2:, 1:-1] + weights_now[2] * padded[:, :-2, 1:-1]
    result = result + weights_now[3] * padded[:, 1:-1, 2:] + weights_now[4] * padded[:, 1:-1, :-2]
    result = (
        result
        + weights_now[5] * vertical[..., :depth_cells]
        + weights_now[6] * vertical[..., depth_cells:]
    )
    return result


def shards(probes, coupling, sensor_cell, sensor_frac, noise_var, owner_slot):
    cells_x = probes.shape[1]
    cells_y = probes.shape[2]
    depth_cells = probes.shape[3]
    tile_x = lax.axis_index("tx")
    tile_y = lax.axis_index("ty")
    total_y = cells_y * lax.axis_size("ty")
    table = shift_table(depth_cells)

    def one_step(number, tracer):
        padded = padded_2(tracer, (("tx", 1), ("ty", 2)), 1)
        return advance(padded, coupling, table)

    tracer = lax.fori_loop(0, STEPS, one_step, probes)
    plane_cells = total_y * depth_cells
    global_x = sensor_cell // plane_cells
    global_y = sensor_cell // depth_cells % total_y
    global_z = sensor_cell % depth_cells
    local_x = global_x - tile_x * cells_x
    local_y = global_y - tile_y * cells_y
    inside = (local_x >= 0) & (local_x < cells_x) & (local_y >= 0) & (local_y < cells_y)
    line_index = jnp.clip(local_x, 0, cells_x - 1) * cells_y + jnp.clip(local_y, 0, cells_y - 1)
    lines = tracer.reshape(tracer.shape[0], cells_x * cells_y, depth_cells)
    picked = jnp.take(lines, line_index, axis=1)
    heights = jnp.arange(depth_cells, dtype=jnp.int32)[None, :]
    below_pick = (heights == global_z[:, None]).astype(jnp.float32)
    above_pick = (heights == global_z[:, None] + 1).astype(jnp.float32)
    below_value = jnp.sum(picked * below_pick[None], axis=2)
    above_value = jnp.sum(picked * above_pick[None], axis=2)
    values = (1.0 - sensor_frac) * below_value + sensor_frac * above_value
    energy = jnp.sum(values * values, axis=0)
    contrib = jnp.where(inside, -energy / noise_var, 0.0)
    ordered = jnp.zeros_like(contrib).at[owner_slot].set(contrib)
    return lax.psum_scatter(ordered, ("probe", "tx", "ty"), scatter_dimension=0, tiled=True)


def solution(mesh):
    in_specs = (P("probe", "tx", "ty", None), P(None, "tx", "ty", None), P(), P(), P(), P())
    out_specs = P(("probe", "tx", "ty"))
    return jax.shard_map(shards, mesh=mesh, in_specs=in_specs, out_specs=out_specs, check_vma=False)
```

profile of v0, /device:TPU:1, one launch (start us, length us, event | category | flops | bytes accessed | tf_op | source)
XLA Modules:
  0.0 665.7 jit_solution(6747191020941262438)
XLA Ops:
  3.8 475.5 %while.10 = (s32[]{:T(128)}, f32[4,32,32,128]{3,2,1,0:T(8,128)}, f32[7,32,32,128]{3,2,1,0:T(8,128)}, f32[128,256]{1,0:T(8,128)S(1)}, s32[]{:T(128)}) while((s32[]{:T(128)}, f32[4,32,32,128]{3,2,1,0:T(8,128)}, f32[7,32,32,128]{3,2,1,0:T(8,128)}, f32[128,256]{1,0:T(8,128)S(1)}, s32[]{:T(128)}) %tuple.37), condition=%wide.region_1.0_spmd, body=%wide.region_0.0_spmd.sunk | while | flops 1619525632 | bytes 62185748 | solution.py:64
  12.3 4.9 fusion.33
  28.0 6.6 fusion.36
  36.3 5.1 collective-permute-start
  43.3 4.9 fusion.33
  59.0 6.6 fusion.36
  67.3 5.1 collective-permute-start
  74.3 4.9 fusion.33
  89.7 6.6 fusion.36
  98.0 5.1 collective-permute-start
  105.0 4.9 fusion.33
  119.3 6.6 fusion.36
  127.5 5.1 collective-permute-start
  134.5 4.9 fusion.33
  148.7 6.6 fusion.36
  157.0 5.1 collective-permute-start
  164.0 4.9 fusion.33
  178.2 6.6 fusion.36
  186.4 5.1 collective-permute-start
  193.4 4.9 fusion.33
  207.6 6.6 fusion.36
  215.9 5.1 collective-permute-start
  237.1 6.6 fusion.36
  245.3 5.1 collective-permute-start
  252.3 4.9 fusion.33
  266.5 6.6 fusion.36
  274.7 5.1 collective-permute-start
  296.0 6.6 fusion.36
  304.2 5.1 collective-permute-start
  325.4 6.6 fusion.36
  333.6 5.1 collective-permute-start
  340.7 4.9 fusion.33
  354.9 6.6 fusion.36
  363.1 5.1 collective-permute-start
  384.3 6.6 fusion.36
  392.6 5.1 collective-permute-start
  399.6 4.9 fusion.33
  413.8 6.6 fusion.36
  422.0 5.1 collective-permute-start
  429.0 4.9 fusion.33
  443.2 6.6 fusion.36
  451.4 5.1 collective-permute-start
  458.5 4.9 fusion.33
  472.7 6.6 fusion.36
  482.8 30.2 %gather_fusion = f32[4096,4,128]{2,1,0:T(4,128)} fusion(f32[4,1024,128]{2,0,1:T(4,128)S(1)} %bitcast.27, s32[4096]{0:T(1024)S(1)} %get-tuple-element.51), kind=kCustom, calls=%fused_computation | custom fusion | bytes 16793600 | tf_op jit(solution)/shard_map/jit(_take)/gather | solution.py:74
  514.3 65.3 %multiply_reduce_fusion.1 = (f32[4096,4]{1,0:T(8,128)S(1)}, f32[4096,4]{1,0:T(8,128)}) fusion(f32[4096,4,128]{2,1,0:T(4,128)} %gather_fusion, f32[4096,128]{1,0:T(8,128)S(1)} %get-tuple-element.54, pred[4096]{0:T(1024)(128)(4,1)S(1)} %compare_and_fusion, f32[4096,128]{1,0:T(8,128)S(1)} %get-tuple-element.55), kind=kLoop, calls=%fused_computation.31 | loop fusion | flops 10452992 | bytes 12718080 | tf_op jit(solution)/shard_map/reduce_sum | solution.py:78
  582.6 15.7 %scatter_custom_fusion = f32[4096]{0:T(1024)S(1)} fusion(s32[4096]{0:T(1024)} %compare_select_fusion.1, f32[4096]{0:T(1024)S(1)} %divide_select_fusion, f32[]{:T(128)} %constant.70.clone.1), kind=kCustom, calls=%fused_computation.65 | custom fusion | bytes 16896 | tf_op jit(solution)/shard_map/scatter | solution.py:83
  598.3 66.9 %all-reduce = f32[4096]{0:T(1024)S(1)} all-reduce(f32[4096]{0:T(1024)S(1)} %scatter_custom_fusion), channel_id=2, replica_groups=mesh['probe'=4,'tx'=8,'ty'=4] {'probe','tx','ty'}, use_global_device_ids=true, to_apply=%region_6.7.clone | all-reduce | flops 4096 | bytes 32768
  (317 shorter events, 244.9 us)
Async XLA Ops:
  5.4 11.8 %collective-permute-start = (f32[4,1,32,128]{3,2,1,0:T(8,128)S(1)}, f32[4,1,32,128]{3,2,1,0:T(8,128)S(1)}, u32[]{:S(2)}, u32[]{:S(2)}) collective-permute-start(f32[4,1,32,128]{3,2,1,0:T(8,128)S(1)} %get-tuple-element.92), channel_id=1, source_target_pairs={{0,4},{4,8},{8,12},{12,16},{16,20},{20,24},{24,28},{1,5},{5,9},{9,... | collective-permute-start | bytes 196616 | tf_op jit(solution)/shard_map/while/body/eval_jaxpr/ppermute | solution.py:14
  10.3 7.1 %collective-permute-start.1 = (f32[4,1,32,128]{3,2,1,0:T(8,128)S(1)}, f32[4,1,32,128]{3,2,1,0:T(8,128)S(1)}, u32[]{:S(2)}, u32[]{:S(2)}) collective-permute-start(f32[4,1,32,128]{3,2,1,0:T(8,128)S(1)} %get-tuple-element.93), channel_id=1, source_target_pairs={{4,0},{8,4},{12,8},{16,12},{20,16},{24,20},{28,24},{5,1},{9,5},{13... | collective-permute-start | bytes 196616 | tf_op jit(solution)/shard_map/while/body/eval_jaxpr/ppermute | solution.py:17
  19.6 6.1 collective-permute-start.2
  22.8 5.3 collective-permute-start.3
  36.3 11.9 %collective-permute-start = (f32[4,1,32,128]{3,2,1,0:T(8,128)S(1)}, f32[4,1,32,128]{3,2,1,0:T(8,128)S(1)}, u32[]{:S(2)}, u32[]{:S(2)}) collective-permute-start(f32[4,1,32,128]{3,2,1,0:T(8,128)S(1)} %get-tuple-element.92), channel_id=1, source_target_pairs={{0,4},{4,8},{8,12},{12,16},{16,20},{20,24},{24,28},{1,5},{5,9},{9,... | collective-permute-start | bytes 196616 | tf_op jit(solution)/shard_map/while/body/eval_jaxpr/ppermute | solution.py:14
  41.3 7.1 %collective-permute-start.1 = (f32[4,1,32,128]{3,2,1,0:T(8,128)S(1)}, f32[4,1,32,128]{3,2,1,0:T(8,128)S(1)}, u32[]{:S(2)}, u32[]{:S(2)}) collective-permute-start(f32[4,1,32,128]{3,2,1,0:T(8,128)S(1)} %get-tuple-element.93), channel_id=1, source_target_pairs={{4,0},{8,4},{12,8},{16,12},{20,16},{24,20},{28,24},{5,1},{9,5},{13... | collective-permute-start | bytes 196616 | tf_op jit(solution)/shard_map/while/body/eval_jaxpr/ppermute | solution.py:17
  50.6 6.1 collective-permute-start.2
  53.8 5.3 collective-permute-start.3
  67.3 11.9 %collective-permute-start = (f32[4,1,32,128]{3,2,1,0:T(8,128)S(1)}, f32[4,1,32,128]{3,2,1,0:T(8,128)S(1)}, u32[]{:S(2)}, u32[]{:S(2)}) collective-permute-start(f32[4,1,32,128]{3,2,1,0:T(8,128)S(1)} %get-tuple-element.92), channel_id=1, source_target_pairs={{0,4},{4,8},{8,12},{12,16},{16,20},{20,24},{24,28},{1,5},{5,9},{9,... | collective-permute-start | bytes 196616 | tf_op jit(solution)/shard_map/while/body/eval_jaxpr/ppermute | solution.py:14
  72.3 7.1 %collective-permute-start.1 = (f32[4,1,32,128]{3,2,1,0:T(8,128)S(1)}, f32[4,1,32,128]{3,2,1,0:T(8,128)S(1)}, u32[]{:S(2)}, u32[]{:S(2)}) collective-permute-start(f32[4,1,32,128]{3,2,1,0:T(8,128)S(1)} %get-tuple-element.93), channel_id=1, source_target_pairs={{4,0},{8,4},{12,8},{16,12},{20,16},{24,20},{28,24},{5,1},{9,5},{13... | collective-permute-start | bytes 196616 | tf_op jit(solution)/shard_map/while/body/eval_jaxpr/ppermute | solution.py:17
  81.6 5.8 collective-permute-start.2
  84.5 5.3 collective-permute-start.3
  98.0 11.9 %collective-permute-start = (f32[4,1,32,128]{3,2,1,0:T(8,128)S(1)}, f32[4,1,32,128]{3,2,1,0:T(8,128)S(1)}, u32[]{:S(2)}, u32[]{:S(2)}) collective-permute-start(f32[4,1,32,128]{3,2,1,0:T(8,128)S(1)} %get-tuple-element.92), channel_id=1, source_target_pairs={{0,4},{4,8},{8,12},{12,16},{16,20},{20,24},{24,28},{1,5},{5,9},{9,... | collective-permute-start | bytes 196616 | tf_op jit(solution)/shard_map/while/body/eval_jaxpr/ppermute | solution.py:14
  103.1 7.1 %collective-permute-start.1 = (f32[4,1,32,128]{3,2,1,0:T(8,128)S(1)}, f32[4,1,32,128]{3,2,1,0:T(8,128)S(1)}, u32[]{:S(2)}, u32[]{:S(2)}) collective-permute-start(f32[4,1,32,128]{3,2,1,0:T(8,128)S(1)} %get-tuple-element.93), channel_id=1, source_target_pairs={{4,0},{8,4},{12,8},{16,12},{20,16},{24,20},{28,24},{5,1},{9,5},{13... | collective-permute-start | bytes 196616 | tf_op jit(solution)/shard_map/while/body/eval_jaxpr/ppermute | solution.py:17
  114.0 5.3 collective-permute-start.3
  127.5 11.9 %collective-permute-start = (f32[4,1,32,128]{3,2,1,0:T(8,128)S(1)}, f32[4,1,32,128]{3,2,1,0:T(8,128)S(1)}, u32[]{:S(2)}, u32[]{:S(2)}) collective-permute-start(f32[4,1,32,128]{3,2,1,0:T(8,128)S(1)} %get-tuple-element.92), channel_id=1, source_target_pairs={{0,4},{4,8},{8,12},{12,16},{16,20},{20,24},{24,28},{1,5},{5,9},{9,... | collective-permute-start | bytes 196616 | tf_op jit(solution)/shard_map/while/body/eval_jaxpr/ppermute | solution.py:14
  132.6 7.1 %collective-permute-start.1 = (f32[4,1,32,128]{3,2,1,0:T(8,128)S(1)}, f32[4,1,32,128]{3,2,1,0:T(8,128)S(1)}, u32[]{:S(2)}, u32[]{:S(2)}) collective-permute-start(f32[4,1,32,128]{3,2,1,0:T(8,128)S(1)} %get-tuple-element.93), channel_id=1, source_target_pairs={{4,0},{8,4},{12,8},{16,12},{20,16},{24,20},{28,24},{5,1},{9,5},{13... | collective-permute-start | bytes 196616 | tf_op jit(solution)/shard_map/while/body/eval_jaxpr/ppermute | solution.py:17
  143.5 5.3 collective-permute-start.3
  157.0 11.9 %collective-permute-start = (f32[4,1,32,128]{3,2,1,0:T(8,128)S(1)}, f32[4,1,32,128]{3,2,1,0:T(8,128)S(1)}, u32[]{:S(2)}, u32[]{:S(2)}) collective-permute-start(f32[4,1,32,128]{3,2,1,0:T(8,128)S(1)} %get-tuple-element.92), channel_id=1, source_target_pairs={{0,4},{4,8},{8,12},{12,16},{16,20},{20,24},{24,28},{1,5},{5,9},{9,... | collective-permute-start | bytes 196616 | tf_op jit(solution)/shard_map/while/body/eval_jaxpr/ppermute | solution.py:14
  162.0 7.1 %collective-permute-start.1 = (f32[4,1,32,128]{3,2,1,0:T(8,128)S(1)}, f32[4,1,32,128]{3,2,1,0:T(8,128)S(1)}, u32[]{:S(2)}, u32[]{:S(2)}) collective-permute-start(f32[4,1,32,128]{3,2,1,0:T(8,128)S(1)} %get-tuple-element.93), channel_id=1, source_target_pairs={{4,0},{8,4},{12,8},{16,12},{20,16},{24,20},{28,24},{5,1},{9,5},{13... | collective-permute-start | bytes 196616 | tf_op jit(solution)/shard_map/while/body/eval_jaxpr/ppermute | solution.py:17
  172.9 5.3 collective-permute-start.3
  186.4 11.9 %collective-permute-start = (f32[4,1,32,128]{3,2,1,0:T(8,128)S(1)}, f32[4,1,32,128]{3,2,1,0:T(8,128)S(1)}, u32[]{:S(2)}, u32[]{:S(2)}) collective-permute-start(f32[4,1,32,128]{3,2,1,0:T(8,128)S(1)} %get-tuple-element.92), channel_id=1, source_target_pairs={{0,4},{4,8},{8,12},{12,16},{16,20},{20,24},{24,28},{1,5},{5,9},{9,... | collective-permute-start | bytes 196616 | tf_op jit(solution)/shard_map/while/body/eval_jaxpr/ppermute | solution.py:14
  191.5 7.1 %collective-permute-start.1 = (f32[4,1,32,128]{3,2,1,0:T(8,128)S(1)}, f32[4,1,32,128]{3,2,1,0:T(8,128)S(1)}, u32[]{:S(2)}, u32[]{:S(2)}) collective-permute-start(f32[4,1,32,128]{3,2,1,0:T(8,128)S(1)} %get-tuple-element.93), channel_id=1, source_target_pairs={{4,0},{8,4},{12,8},{16,12},{20,16},{24,20},{28,24},{5,1},{9,5},{13... | collective-permute-start | bytes 196616 | tf_op jit(solution)/shard_map/while/body/eval_jaxpr/ppermute | solution.py:17
  202.4 5.3 collective-permute-start.3
  215.9 11.9 %collective-permute-start = (f32[4,1,32,128]{3,2,1,0:T(8,128)S(1)}, f32[4,1,32,128]{3,2,1,0:T(8,128)S(1)}, u32[]{:S(2)}, u32[]{:S(2)}) collective-permute-start(f32[4,1,32,128]{3,2,1,0:T(8,128)S(1)} %get-tuple-element.92), channel_id=1, source_target_pairs={{0,4},{4,8},{8,12},{12,16},{16,20},{20,24},{24,28},{1,5},{5,9},{9,... | collective-permute-start | bytes 196616 | tf_op jit(solution)/shard_map/while/body/eval_jaxpr/ppermute | solution.py:14
  220.9 7.1 %collective-permute-start.1 = (f32[4,1,32,128]{3,2,1,0:T(8,128)S(1)}, f32[4,1,32,128]{3,2,1,0:T(8,128)S(1)}, u32[]{:S(2)}, u32[]{:S(2)}) collective-permute-start(f32[4,1,32,128]{3,2,1,0:T(8,128)S(1)} %get-tuple-element.93), channel_id=1, source_target_pairs={{4,0},{8,4},{12,8},{16,12},{20,16},{24,20},{28,24},{5,1},{9,5},{13... | collective-permute-start | bytes 196616 | tf_op jit(solution)/shard_map/while/body/eval_jaxpr/ppermute | solution.py:17
  231.8 5.3 collective-permute-start.3
  245.3 11.9 %collective-permute-start = (f32[4,1,32,128]{3,2,1,0:T(8,128)S(1)}, f32[4,1,32,128]{3,2,1,0:T(8,128)S(1)}, u32[]{:S(2)}, u32[]{:S(2)}) collective-permute-start(f32[4,1,32,128]{3,2,1,0:T(8,128)S(1)} %get-tuple-element.92), channel_id=1, source_target_pairs={{0,4},{4,8},{8,12},{12,16},{16,20},{20,24},{24,28},{1,5},{5,9},{9,... | collective-permute-start | bytes 196616 | tf_op jit(solution)/shard_map/while/body/eval_jaxpr/ppermute | solution.py:14
  250.4 7.1 %collective-permute-start.1 = (f32[4,1,32,128]{3,2,1,0:T(8,128)S(1)}, f32[4,1,32,128]{3,2,1,0:T(8,128)S(1)}, u32[]{:S(2)}, u32[]{:S(2)}) collective-permute-start(f32[4,1,32,128]{3,2,1,0:T(8,128)S(1)} %get-tuple-element.93), channel_id=1, source_target_pairs={{4,0},{8,4},{12,8},{16,12},{20,16},{24,20},{28,24},{5,1},{9,5},{13... | collective-permute-start | bytes 196616 | tf_op jit(solution)/shard_map/while/body/eval_jaxpr/ppermute | solution.py:17
  261.3 5.3 collective-permute-start.3
  274.7 11.9 %collective-permute-start = (f32[4,1,32,128]{3,2,1,0:T(8,128)S(1)}, f32[4,1,32,128]{3,2,1,0:T(8,128)S(1)}, u32[]{:S(2)}, u32[]{:S(2)}) collective-permute-start(f32[4,1,32,128]{3,2,1,0:T(8,128)S(1)} %get-tuple-element.92), channel_id=1, source_target_pairs={{0,4},{4,8},{8,12},{12,16},{16,20},{20,24},{24,28},{1,5},{5,9},{9,... | collective-permute-start | bytes 196616 | tf_op jit(solution)/shard_map/while/body/eval_jaxpr/ppermute | solution.py:14
  279.8 7.1 %collective-permute-start.1 = (f32[4,1,32,128]{3,2,1,0:T(8,128)S(1)}, f32[4,1,32,128]{3,2,1,0:T(8,128)S(1)}, u32[]{:S(2)}, u32[]{:S(2)}) collective-permute-start(f32[4,1,32,128]{3,2,1,0:T(8,128)S(1)} %get-tuple-element.93), channel_id=1, source_target_pairs={{4,0},{8,4},{12,8},{16,12},{20,16},{24,20},{28,24},{5,1},{9,5},{13... | collective-permute-start | bytes 196616 | tf_op jit(solution)/shard_map/while/body/eval_jaxpr/ppermute | solution.py:17
  290.7 5.3 collective-permute-start.3
  304.2 11.9 %collective-permute-start = (f32[4,1,32,128]{3,2,1,0:T(8,128)S(1)}, f32[4,1,32,128]{3,2,1,0:T(8,128)S(1)}, u32[]{:S(2)}, u32[]{:S(2)}) collective-permute-start(f32[4,1,32,128]{3,2,1,0:T(8,128)S(1)} %get-tuple-element.92), channel_id=1, source_target_pairs={{0,4},{4,8},{8,12},{12,16},{16,20},{20,24},{24,28},{1,5},{5,9},{9,... | collective-permute-start | bytes 196616 | tf_op jit(solution)/shard_map/while/body/eval_jaxpr/ppermute | solution.py:14
  309.3 7.1 %collective-permute-start.1 = (f32[4,1,32,128]{3,2,1,0:T(8,128)S(1)}, f32[4,1,32,128]{3,2,1,0:T(8,128)S(1)}, u32[]{:S(2)}, u32[]{:S(2)}) collective-permute-start(f32[4,1,32,128]{3,2,1,0:T(8,128)S(1)} %get-tuple-element.93), channel_id=1, source_target_pairs={{4,0},{8,4},{12,8},{16,12},{20,16},{24,20},{28,24},{5,1},{9,5},{13... | collective-permute-start | bytes 196616 | tf_op jit(solution)/shard_map/while/body/eval_jaxpr/ppermute | solution.py:17
  320.2 5.3 collective-permute-start.3
  333.6 11.9 %collective-permute-start = (f32[4,1,32,128]{3,2,1,0:T(8,128)S(1)}, f32[4,1,32,128]{3,2,1,0:T(8,128)S(1)}, u32[]{:S(2)}, u32[]{:S(2)}) collective-permute-start(f32[4,1,32,128]{3,2,1,0:T(8,128)S(1)} %get-tuple-element.92), channel_id=1, source_target_pairs={{0,4},{4,8},{8,12},{12,16},{16,20},{20,24},{24,28},{1,5},{5,9},{9,... | collective-permute-start | bytes 196616 | tf_op jit(solution)/shard_map/while/body/eval_jaxpr/ppermute | solution.py:14
  338.7 7.1 %collective-permute-start.1 = (f32[4,1,32,128]{3,2,1,0:T(8,128)S(1)}, f32[4,1,32,128]{3,2,1,0:T(8,128)S(1)}, u32[]{:S(2)}, u32[]{:S(2)}) collective-permute-start(f32[4,1,32,128]{3,2,1,0:T(8,128)S(1)} %get-tuple-element.93), channel_id=1, source_target_pairs={{4,0},{8,4},{12,8},{16,12},{20,16},{24,20},{28,24},{5,1},{9,5},{13... | collective-permute-start | bytes 196616 | tf_op jit(solution)/shard_map/while/body/eval_jaxpr/ppermute | solution.py:17
  349.6 5.3 collective-permute-start.3
  363.1 11.9 %collective-permute-start = (f32[4,1,32,128]{3,2,1,0:T(8,128)S(1)}, f32[4,1,32,128]{3,2,1,0:T(8,128)S(1)}, u32[]{:S(2)}, u32[]{:S(2)}) collective-permute-start(f32[4,1,32,128]{3,2,1,0:T(8,128)S(1)} %get-tuple-element.92), channel_id=1, source_target_pairs={{0,4},{4,8},{8,12},{12,16},{16,20},{20,24},{24,28},{1,5},{5,9},{9,... | collective-permute-start | bytes 196616 | tf_op jit(solution)/shard_map/while/body/eval_jaxpr/ppermute | solution.py:14
  368.2 7.1 %collective-permute-start.1 = (f32[4,1,32,128]{3,2,1,0:T(8,128)S(1)}, f32[4,1,32,128]{3,2,1,0:T(8,128)S(1)}, u32[]{:S(2)}, u32[]{:S(2)}) collective-permute-start(f32[4,1,32,128]{3,2,1,0:T(8,128)S(1)} %get-tuple-element.93), channel_id=1, source_target_pairs={{4,0},{8,4},{12,8},{16,12},{20,16},{24,20},{28,24},{5,1},{9,5},{13... | collective-permute-start | bytes 196616 | tf_op jit(solution)/shard_map/while/body/eval_jaxpr/ppermute | solution.py:17
  379.1 5.3 collective-permute-start.3
  392.6 11.9 %collective-permute-start = (f32[4,1,32,128]{3,2,1,0:T(8,128)S(1)}, f32[4,1,32,128]{3,2,1,0:T(8,128)S(1)}, u32[]{:S(2)}, u32[]{:S(2)}) collective-permute-start(f32[4,1,32,128]{3,2,1,0:T(8,128)S(1)} %get-tuple-element.92), channel_id=1, source_target_pairs={{0,4},{4,8},{8,12},{12,16},{16,20},{20,24},{24,28},{1,5},{5,9},{9,... | collective-permute-start | bytes 196616 | tf_op jit(solution)/shard_map/while/body/eval_jaxpr/ppermute | solution.py:14
  397.6 7.1 %collective-permute-start.1 = (f32[4,1,32,128]{3,2,1,0:T(8,128)S(1)}, f32[4,1,32,128]{3,2,1,0:T(8,128)S(1)}, u32[]{:S(2)}, u32[]{:S(2)}) collective-permute-start(f32[4,1,32,128]{3,2,1,0:T(8,128)S(1)} %get-tuple-element.93), channel_id=1, source_target_pairs={{4,0},{8,4},{12,8},{16,12},{20,16},{24,20},{28,24},{5,1},{9,5},{13... | collective-permute-start | bytes 196616 | tf_op jit(solution)/shard_map/while/body/eval_jaxpr/ppermute | solution.py:17
  422.0 11.9 %collective-permute-start = (f32[4,1,32,128]{3,2,1,0:T(8,128)S(1)}, f32[4,1,32,128]{3,2,1,0:T(8,128)S(1)}, u32[]{:S(2)}, u32[]{:S(2)}) collective-permute-start(f32[4,1,32,128]{3,2,1,0:T(8,128)S(1)} %get-tuple-element.92), channel_id=1, source_target_pairs={{0,4},{4,8},{8,12},{12,16},{16,20},{20,24},{24,28},{1,5},{5,9},{9,... | collective-permute-start | bytes 196616 | tf_op jit(solution)/shard_map/while/body/eval_jaxpr/ppermute | solution.py:14
  427.1 7.1 %collective-permute-start.1 = (f32[4,1,32,128]{3,2,1,0:T(8,128)S(1)}, f32[4,1,32,128]{3,2,1,0:T(8,128)S(1)}, u32[]{:S(2)}, u32[]{:S(2)}) collective-permute-start(f32[4,1,32,128]{3,2,1,0:T(8,128)S(1)} %get-tuple-element.93), channel_id=1, source_target_pairs={{4,0},{8,4},{12,8},{16,12},{20,16},{24,20},{28,24},{5,1},{9,5},{13... | collective-permute-start | bytes 196616 | tf_op jit(solution)/shard_map/while/body/eval_jaxpr/ppermute | solution.py:17
  451.4 11.9 %collective-permute-start = (f32[4,1,32,128]{3,2,1,0:T(8,128)S(1)}, f32[4,1,32,128]{3,2,1,0:T(8,128)S(1)}, u32[]{:S(2)}, u32[]{:S(2)}) collective-permute-start(f32[4,1,32,128]{3,2,1,0:T(8,128)S(1)} %get-tuple-element.92), channel_id=1, source_target_pairs={{0,4},{4,8},{8,12},{12,16},{16,20},{20,24},{24,28},{1,5},{5,9},{9,... | collective-permute-start | bytes 196616 | tf_op jit(solution)/shard_map/while/body/eval_jaxpr/ppermute | solution.py:14
  456.5 7.1 %collective-permute-start.1 = (f32[4,1,32,128]{3,2,1,0:T(8,128)S(1)}, f32[4,1,32,128]{3,2,1,0:T(8,128)S(1)}, u32[]{:S(2)}, u32[]{:S(2)}) collective-permute-start(f32[4,1,32,128]{3,2,1,0:T(8,128)S(1)} %get-tuple-element.93), channel_id=1, source_target_pairs={{4,0},{8,4},{12,8},{16,12},{20,16},{24,20},{28,24},{5,1},{9,5},{13... | collective-permute-start | bytes 196616 | tf_op jit(solution)/shard_map/while/body/eval_jaxpr/ppermute | solution.py:17
  (52 other events, 198.2 us)
where the time goes:
time: 668 us; the launch traced here: 666 us
  other arithmetic  173 us (26%)
  starting transfers between devices  163 us (24%)
  local copies, waits for them, and re-layouts  144 us (22%)
  matrix products  78.9 us (12%)
  blocking collectives  66.9 us (10%)
  waiting for transfers between devices  38.1 us (6%)
    ppermute x32, starting transfers between devices, padded_2(): lax.ppermute(lax.slice_in_dim(block, block.shape[dim] - width, None, axis...  112 us
    add x16, other arithmetic, advance(): result + weights_now[5] * vertical[..., :depth_cells]  106 us
    dot_general x16, matrix products, advance(): jnp.einsum('pxyz,zw->pxyw', centre_cells, table, precision=lax.Precision....  78.9 us
    unnamed x1, blocking collectives  66.9 us
    reduce_sum x1, other arithmetic, shards(): below_value = jnp.sum(picked * below_pick[None], axis=2)  65.3 us
    ppermute x32, starting transfers between devices, padded_2(): lax.ppermute(lax.slice_in_dim(block, 0, width, axis=dim), axis, backward)  51.4 us
    while x112, local copies, waits for them, and re-layouts  50.8 us
    ppermute x32, waiting for transfers between devices, padded_2(): lax.ppermute(lax.slice_in_dim(block, 0, width, axis=dim), axis, backward)  38 us
  transfers between devices with their start and end apart: 64, of which 16 were waited for; matrix products, arithmetic and copies ran while one was open for 16% of the time, Pallas kernels for 0%

commit v1 on v0

v1 whole, which is shorter than its diff:
```python
import functools

import jax
import jax.numpy as jnp
from jax import lax
from jax.experimental import pallas as pl
from jax.experimental.pallas import tpu as pltpu
from jax.sharding import PartitionSpec as P

STEPS = 16
MESH = pl.DeviceIdType.MESH
GROUP = 2
LEAD = 8


def stencil_kernel(
    np_, nx, ny, probes_hbm, coup_hbm, out_hbm, va, vb, c, ysend, yrecv, load_sem, coup_sem, send_sem, recv_sem
):
    bufs = (va, vb)
    planes = nx + 2
    tx, ty = lax.axis_index("tx"), lax.axis_index("ty")
    ntx, nty = lax.axis_size("tx"), lax.axis_size("ty")
    has = (tx > 0, tx < ntx - 1, ty > 0, ty < nty - 1)
    where = ({"tx": tx - 1}, {"tx": tx + 1}, {"ty": ty - 1}, {"ty": ty + 1})

    loads = []
    for p in range(np_):
        cp = pltpu.make_async_copy(
            probes_hbm.at[p], va.at[pl.ds(p * planes + 1, nx), pl.ds(LEAD, ny)], load_sem.at[p]
        )
        cp.start()
        loads.append(cp)
    cload = []
    for k in range(7):
        cp = pltpu.make_async_copy(coup_hbm.at[k], c.at[k], coup_sem.at[k])
        cp.start()
        cload.append(cp)

    zrow = jnp.zeros((8, 128), jnp.float32)
    for buf in bufs:
        for p in range(np_):
            for q in (p * planes, p * planes + nx + 1):
                for t in range(ny // 8):
                    buf[q, pl.ds(LEAD + 8 * t, 8)] = zrow

            def zero_rows(i, _, buf=buf, p=p):
                buf[p * planes + 1 + i, pl.ds(0, 8)] = zrow
                buf[p * planes + 1 + i, pl.ds(LEAD + ny, 8)] = zrow
                return 0

            lax.fori_loop(0, nx, zero_rows, 0)

    barrier = pltpu.get_barrier_semaphore()
    for d in range(4):

        @pl.when(has[d])
        def _(d=d):
            pl.semaphore_signal(barrier, inc=1, device_id=where[d], device_id_type=MESH)

    pl.semaphore_wait(barrier, sum(h.astype(jnp.int32) for h in has))

    def copy(d, par, p):
        v = bufs[par]
        if d < 2:
            src = v.at[p * planes + (1 if d == 0 else nx), pl.ds(LEAD, ny)]
            dst = v.at[p * planes + (nx + 1 if d == 0 else 0), pl.ds(LEAD, ny)]
        else:
            src = ysend.at[par, d - 2, p]
            dst = yrecv.at[par, d - 2, p]
        return pltpu.make_async_remote_copy(
            src_ref=src,
            dst_ref=dst,
            send_sem=send_sem.at[par, d, p],
            recv_sem=recv_sem.at[par, d, p],
            device_id=where[d],
            device_id_type=MESH,
        )

    opposite = (1, 0, 3, 2)

    def pack(par, p):
        v = bufs[par]
        ysend[par, 0, p] = v[pl.ds(p * planes + 1, nx), LEAD, :]
        ysend[par, 1, p] = v[pl.ds(p * planes + 1, nx), LEAD + ny - 1, :]

    def send(par, p):
        for d in (2, 3, 0, 1):

            @pl.when(has[d])
            def _(d=d):
                copy(d, par, p).start()

    def wait_send(par, p):
        for d in range(4):

            @pl.when(has[d])
            def _(d=d):
                copy(d, par, p).wait_send()

    def receive(par, p):
        v = bufs[par]
        for d in range(4):

            @pl.when(has[opposite[d]])
            def _(d=d):
                copy(d, par, p).wait_recv()
                if d == 2:
                    v[pl.ds(p * planes + 1, nx), LEAD + ny, :] = yrecv[par, 0, p]
                if d == 3:
                    v[pl.ds(p * planes + 1, nx), LEAD - 1, :] = yrecv[par, 1, p]

    for p in range(np_):
        loads[p].wait()
        pack(0, p)
        send(0, p)
    for k in range(7):
        cload[k].wait()
    lane = lax.broadcasted_iota(jnp.int32, (8, 128), 1)

    def clip_edges(i, _):
        for t in range(ny // 8):
            rows = pl.ds(8 * t, 8)
            c[5, i, rows] = jnp.where(lane == 127, 0.0, c[5, i, rows])
            c[6, i, rows] = jnp.where(lane == 0, 0.0, c[6, i, rows])
        return 0

    lax.fori_loop(0, nx, clip_edges, 0)

    def compute(group, par):
        src, dst = bufs[par], bufs[1 - par]
        tiles = ny // 8

        def at(p, plane, t, off=0):
            return src[p * planes + plane, pl.ds(LEAD + 8 * t + off, 8)]

        def body(i, carry):
            prev, cur = carry
            nxt = []
            for t in range(tiles):
                coef = [c[k, i, pl.ds(8 * t, 8)] for k in range(7)]
                for g, p in enumerate(group):
                    n = t * len(group) + g
                    v = cur[n]
                    ahead = at(p, i + 2, t)
                    up = at(p, i + 1, t, 1)
                    down = at(p, i + 1, t, -1)
                    r = coef[0] * v
                    r = r + (coef[1] * ahead + coef[2] * prev[n])
                    r = r + (coef[3] * up + coef[4] * down)
                    r = r + (coef[5] * pltpu.roll(v, 127, 1) + coef[6] * pltpu.roll(v, 1, 1))
                    dst[p * planes + i + 1, pl.ds(LEAD + 8 * t, 8)] = r
                    nxt.append(ahead)
            return cur, tuple(nxt)

        order = [(t, p) for t in range(tiles) for p in group]
        prev = tuple(at(p, 0, t) for t, p in order)
        cur = tuple(at(p, 1, t) for t, p in order)
        lax.fori_loop(0, nx, body, (prev, cur))

    groups = [tuple(range(g, g + GROUP)) for g in range(0, np_, GROUP)]

    def two_steps(it, _):
        for par in range(2):
            for group in groups:
                for p in group:
                    receive(par, p)
                if par == 1:
                    for p in group:
                        wait_send(1 - par, p)
                else:

                    @pl.when(it > 0)
                    def _():
                        for p in group:
                            wait_send(1 - par, p)

                compute(group, par)
                if par == 0:
                    for p in group:
                        pack(1 - par, p)
                        send(1 - par, p)
                else:

                    @pl.when(it < STEPS // 2 - 1)
                    def _():
                        for p in group:
                            pack(1 - par, p)
                            send(1 - par, p)

        return 0

    lax.fori_loop(0, STEPS // 2, two_steps, 0)
    for p in range(np_):
        wait_send(1, p)
        cp = pltpu.make_async_copy(
            va.at[pl.ds(p * planes + 1, nx), pl.ds(LEAD, ny)],
            out_hbm.at[:, :, pl.ds(p * 128, 128)],
            load_sem.at[p],
        )
        cp.start()
    for p in range(np_):
        pltpu.make_async_copy(
            va.at[pl.ds(p * planes + 1, nx), pl.ds(LEAD, ny)],
            out_hbm.at[:, :, pl.ds(p * 128, 128)],
            load_sem.at[p],
        ).wait()


def stencil(probes, coupling):
    np_, nx, ny, nz = probes.shape
    planes = nx + 2
    field = pltpu.VMEM((np_ * planes, ny + 16, nz), jnp.float32)
    face = pltpu.VMEM((2, 2, np_, nx, nz), jnp.float32)
    return pl.pallas_call(
        functools.partial(stencil_kernel, np_, nx, ny),
        out_shape=jax.ShapeDtypeStruct((nx, ny, np_ * nz), jnp.float32),
        in_specs=[pl.BlockSpec(memory_space=pl.ANY)] * 2,
        out_specs=pl.BlockSpec(memory_space=pl.ANY),
        scratch_shapes=[
            field,
            field,
            pltpu.VMEM(coupling.shape, jnp.float32),
            face,
            face,
            pltpu.SemaphoreType.DMA((np_,)),
            pltpu.SemaphoreType.DMA((7,)),
            pltpu.SemaphoreType.DMA((2, 4, np_)),
            pltpu.SemaphoreType.DMA((2, 4, np_)),
        ],
        compiler_params=pltpu.CompilerParams(collective_id=0, has_side_effects=True, vmem_limit_bytes=32 << 20),
        name="stencil",
    )(probes, coupling)


def shards(probes, coupling, sensor_cell, sensor_frac, noise_var, owner_slot):
    cells_x = probes.shape[1]
    cells_y = probes.shape[2]
    depth_cells = probes.shape[3]
    tile_x = lax.axis_index("tx")
    tile_y = lax.axis_index("ty")
    total_y = cells_y * lax.axis_size("ty")
    tracer = stencil(probes, coupling)
    plane_cells = total_y * depth_cells
    global_x = sensor_cell // plane_cells
    global_y = sensor_cell // depth_cells % total_y
    global_z = sensor_cell % depth_cells
    local_x = global_x - tile_x * cells_x
    local_y = global_y - tile_y * cells_y
    inside = (local_x >= 0) & (local_x < cells_x) & (local_y >= 0) & (local_y < cells_y)
    line_index = jnp.clip(local_x, 0, cells_x - 1) * cells_y + jnp.clip(local_y, 0, cells_y - 1)
    lines = tracer.reshape(cells_x * cells_y, 4, depth_cells)
    picked = jnp.take(lines, line_index, axis=0)
    heights = jnp.arange(depth_cells, dtype=jnp.int32)[None, :]
    below_pick = (heights == global_z[:, None]).astype(jnp.float32)
    above_pick = (heights == global_z[:, None] + 1).astype(jnp.float32)
    below_value = jnp.sum(picked * below_pick[:, None], axis=2)
    above_value = jnp.sum(picked * above_pick[:, None], axis=2)
    values = (1.0 - sensor_frac)[:, None] * below_value + sensor_frac[:, None] * above_value
    energy = jnp.sum(values * values, axis=1)
    contrib = jnp.where(inside, -energy / noise_var, 0.0)
    ordered = jnp.zeros_like(contrib).at[owner_slot].set(contrib)
    return lax.psum_scatter(ordered, ("probe", "tx", "ty"), scatter_dimension=0, tiled=True)


def solution(mesh):
    in_specs = (P("probe", "tx", "ty", None), P(None, "tx", "ty", None), P(), P(), P(), P())
    out_specs = P(("probe", "tx", "ty"))
    return jax.shard_map(shards, mesh=mesh, in_specs=in_specs, out_specs=out_specs, check_vma=False)
```

time: 668 us -> 298 us (0.45)
  starting transfers between devices: 163 us -> 0 us
  Pallas kernels: 0 us -> 107 us
  other arithmetic: 173 us -> 71.7 us
  local copies, waits for them, and re-layouts: 144 us -> 54.4 us
  matrix products: 78.9 us -> 0 us
  waiting for transfers between devices: 38.1 us -> 0 us
    ppermute x64 -> x0, starting transfers between devices: 163 us -> none  [the longest x32 112 us: padded_2(): lax.ppermute(lax.slice_in_dim(block, block.shape[dim] - width, None, axis...]
    pallas_call x0 -> x1, Pallas kernels: none -> 107 us  [stencil(): pl.pallas_call(functools.partial(stencil_kernel, np_, nx, ny), out_shape=...]
    add x17 -> x0, other arithmetic: 106 us -> none  [the longest x16 106 us: advance(): result + weights_now[5] * vertical[..., :depth_cells]]
    dot_general x16 -> x0, matrix products: 78.9 us -> none  [advance(): jnp.einsum('pxyz,zw->pxyw', centre_cells, table, precision=lax.Precision....]
    while x113 -> x0, local copies, waits for them, and re-layouts: 54.1 us -> none
    ppermute x64 -> x0, waiting for transfers between devices: 38.1 us -> none  [the longest x32 38 us: padded_2(): lax.ppermute(lax.slice_in_dim(block, 0, width, axis=dim), axis, backward)]
    mul x16 -> x0, local copies, waits for them, and re-layouts: 25.2 us -> none  [advance(): result = weights_now[0] * centre_cells]
    slice x32 -> x0, local copies, waits for them, and re-layouts: 12.1 us -> none  [padded_2(): lax.slice_in_dim(block, 0, width, axis=dim)]
  transfers between devices with their start and end apart: 64 -> 0, of which waited for: 16 -> 0; matrix products, arithmetic and copies ran while one was open for 16% -> 0% of each run, Pallas kernels for 0% -> 0%
where the time goes in v1:
time: 298 us
  Pallas kernels  107 us (36%)
  other arithmetic  71.7 us (24%)
  blocking collectives  65.1 us (22%)
  local copies, waits for them, and re-layouts  54.4 us (18%)
    pallas_call x1, Pallas kernels, stencil(): pl.pallas_call(functools.partial(stencil_kernel, np_, nx, ny), out_shape=...  107 us
    reduce_sum x1, other arithmetic, shards(): below_value = jnp.sum(picked * below_pick[:, None], axis=2)  66.6 us
    unnamed x1, blocking collectives  65.1 us
    gather x1, local copies, waits for them, and re-layouts, shards(): picked = jnp.take(lines, line_index, axis=0)  31.9 us
    scatter x1, local copies, waits for them, and re-layouts, shards(): ordered = jnp.zeros_like(contrib).at[owner_slot].set(contrib)  15.5 us

profile of v1, /device:TPU:1, one launch (start us, length us, event | category | flops | bytes accessed | tf_op | source)
XLA Modules:
  0.0 297.8 jit_solution(14999702702371204859)
XLA Ops:
  0.0 0.8 broadcast_add_fusion
  0.8 0.0 copy-start
  0.8 4.2 %fusion = (f32[4096,128]{1,0:T(8,128)}, f32[4096,128]{1,0:T(8,128)}) fusion(s32[4096]{0:T(1024)S(1)} %get-tuple-element.8, s32[4096]{0:T(1024)S(1)} %get-tuple-element.7), kind=kLoop, calls=%fused_computation.6 | loop fusion | flops 2097152 | bytes 4227072 | tf_op jit(solution)/shard_map/convert_element_type | solution.py:254
  5.0 0.0 copy-done
  5.0 0.0 copy-start.1
  5.0 1.6 copy-done.1
  6.6 106.6 %stencil.1 = f32[32,32,512]{2,1,0:T(8,128)S(1)} custom-call(f32[4,32,32,128]{3,2,1,0:T(8,128)S(1)} %copy-done.1, f32[7,32,32,128]{3,2,1,0:T(8,128)S(1)} %copy-done), custom_call_target="tpu_custom_call" | custom-call | tf_op jit(solution)/shard_map/stencil/pallas_call | solution.py:214
  113.2 1.7 reshape.47
  114.9 0.0 copy-start.4
  114.9 0.0 copy-start.2
  114.9 31.9 %gather_fusion = f32[4096,4,128]{2,1,0:T(4,128)} fusion(f32[1024,4,128]{2,1,0:T(4,128)} %reshape.47, s32[4096]{0:T(1024)S(1)} %get-tuple-element.9), kind=kCustom, calls=%fused_computation | custom fusion | bytes 16793600 | tf_op jit(solution)/shard_map/jit(_take)/gather | solution.py:252
  146.8 0.0 copy-done.4
  146.8 0.0 copy-done.2
  146.9 66.6 %multiply_reduce_fusion.1 = (f32[4096,4]{1,0:T(8,128)}, f32[4096,4]{1,0:T(8,128)}) fusion(f32[4096,4,128]{2,1,0:T(4,128)} %gather_fusion, f32[4096,128]{1,0:T(8,128)S(1)} %copy-done.2, pred[4096]{0:T(1024)(128)(4,1)S(1)} %compare_and_fusion, f32[4096,128]{1,0:T(8,128)} %get-tuple-element.11), kind=kLoop, calls=%fused_computation.3 | loop fusion | flops 10452992 | bytes 12718080 | tf_op jit(solution)/shard_map/reduce_sum | solution.py:256
  213.4 0.0 copy-start.3
  213.4 0.0 copy-start.5
  213.4 0.0 copy-start.7
  213.4 0.0 copy-start.6
  213.4 2.4 copy.12
  215.8 0.0 copy-done.3
  215.8 0.6 copy.13
  216.4 0.0 copy-done.5
  216.5 0.1 multiply_reduce_fusion.2
  216.5 0.0 copy-done.7
  216.6 0.0 copy-done.6
  216.6 15.5 %scatter_custom_fusion = f32[4096]{0:T(1024)S(1)} fusion(s32[4096]{0:T(1024)S(1)} %compare_select_fusion.1, f32[4096]{0:T(1024)S(1)} %divide_select_fusion, f32[]{:T(128)} %constant.64.clone.1), kind=kCustom, calls=%fused_computation.34 | custom fusion | bytes 16388 | tf_op jit(solution)/shard_map/scatter | solution.py:261
  232.1 65.1 %all-reduce = f32[4096]{0:T(1024)S(1)} all-reduce(f32[4096]{0:T(1024)S(1)} %scatter_custom_fusion), channel_id=2, replica_groups=mesh['probe'=4,'tx'=8,'ty'=4] {'probe','tx','ty'}, use_global_device_ids=true, to_apply=%region_4.5.clone | all-reduce | flops 4096 | bytes 32768
  297.2 0.6 dynamic-slice
  (4 shorter events, 0.1 us)
Async XLA Ops:
  0.8 4.2 %copy-start = (f32[7,32,32,128]{3,2,1,0:T(8,128)S(1)}, f32[7,32,32,128]{3,2,1,0:T(8,128)}, u32[]{:S(2)}) copy-start(f32[7,32,32,128]{3,2,1,0:T(8,128)} %coup_hbm.1) | copy-start | bytes 11010052
  5.0 1.6 copy-start.1
  114.9 31.9 %copy-start.4 = (s32[4096]{0:T(1024)S(1)}, s32[4096]{0:T(1024)}, u32[]{:S(2)}) copy-start(s32[4096]{0:T(1024)} %param.8) | copy-start | bytes 49156
  114.9 31.9 %copy-start.2 = (f32[4096,128]{1,0:T(8,128)S(1)}, f32[4096,128]{1,0:T(8,128)}, u32[]{:S(2)}) copy-start(f32[4096,128]{1,0:T(8,128)} %get-tuple-element.10) | copy-start | bytes 6291460
  213.4 2.4 copy-start.3
  213.4 3.0 %copy-start.5 = (f32[4096]{0:T(1024)S(1)}, f32[4096]{0:T(1024)}, u32[]{:S(2)}) copy-start(f32[4096]{0:T(1024)} %param.9) | copy-start | bytes 49156
  213.4 3.1 %copy-start.7 = (f32[4096]{0:T(1024)S(1)}, f32[4096]{0:T(1024)}, u32[]{:S(2)}) copy-start(f32[4096]{0:T(1024)} %param.10) | copy-start | bytes 49156
  213.4 3.1 %copy-start.6 = (s32[4096]{0:T(1024)S(1)}, s32[4096]{0:T(1024)}, u32[]{:S(2)}) copy-start(s32[4096]{0:T(1024)} %param.11) | copy-start | bytes 49156

commit v2 on v1

--- a/solution.py
+++ b/solution.py
@@ -11,13 +11,17 @@
 MESH = pl.DeviceIdType.MESH
 GROUP = 2
 LEAD = 8
+UNROLL = 4
+CHUNK = 320
 
 
 def stencil_kernel(
     np_, nx, ny, probes_hbm, coup_hbm, out_hbm, va, vb, c, ysend, yrecv, load_sem, coup_sem, send_sem, recv_sem
 ):
+    planes = nx + 2
+    rows = ny + 2 * LEAD
     bufs = (va, vb)
-    planes = nx + 2
+    flat = tuple(v.reshape(np_ * planes * rows, 128) for v in bufs)
     tx, ty = lax.axis_index("tx"), lax.axis_index("ty")
     ntx, nty = lax.axis_size("tx"), lax.axis_size("ty")
     has = (tx > 0, tx < ntx - 1, ty > 0, ty < nty - 1)
@@ -78,10 +82,13 @@
 
     opposite = (1, 0, 3, 2)
 
+    def face(par, p, row):
+        return flat[par], pl.ds((p * planes + 1) * rows + row, nx, stride=rows)
+
     def pack(par, p):
-        v = bufs[par]
-        ysend[par, 0, p] = v[pl.ds(p * planes + 1, nx), LEAD, :]
-        ysend[par, 1, p] = v[pl.ds(p * planes + 1, nx), LEAD + ny - 1, :]
+        for side, row in enumerate((LEAD, LEAD + ny - 1)):
+            ref, lines = face(par, p, row)
+            ysend[par, side, p] = ref[lines, :]
 
     def send(par, p):
         for d in (2, 3, 0, 1):
@@ -98,16 +105,14 @@
                 copy(d, par, p).wait_send()
 
     def receive(par, p):
-        v = bufs[par]
         for d in range(4):
 
             @pl.when(has[opposite[d]])
             def _(d=d):
                 copy(d, par, p).wait_recv()
-                if d == 2:
-                    v[pl.ds(p * planes + 1, nx), LEAD + ny, :] = yrecv[par, 0, p]
-                if d == 3:
-                    v[pl.ds(p * planes + 1, nx), LEAD - 1, :] = yrecv[par, 1, p]
+                if d >= 2:
+                    ref, at = face(par, p, LEAD + ny if d == 2 else LEAD - 1)
+                    ref[at, :] = yrecv[par, d - 2, p]
 
     for p in range(np_):
         loads[p].wait()
@@ -133,8 +138,7 @@
         def at(p, plane, t, off=0):
             return src[p * planes + plane, pl.ds(LEAD + 8 * t + off, 8)]
 
-        def body(i, carry):
-            prev, cur = carry
+        def one(i, prev, cur):
             nxt = []
             for t in range(tiles):
                 coef = [c[k, i, pl.ds(8 * t, 8)] for k in range(7)]
@@ -152,10 +156,15 @@
                     nxt.append(ahead)
             return cur, tuple(nxt)
 
+        def body(block, carry):
+            for u in range(UNROLL):
+                carry = one(block * UNROLL + u, *carry)
+            return carry
+
         order = [(t, p) for t in range(tiles) for p in group]
         prev = tuple(at(p, 0, t) for t, p in order)
         cur = tuple(at(p, 1, t) for t, p in order)
-        lax.fori_loop(0, nx, body, (prev, cur))
+        lax.fori_loop(0, nx // UNROLL, body, (prev, cur))
 
     groups = [tuple(range(g, g + GROUP)) for g in range(0, np_, GROUP)]
 
@@ -209,7 +218,7 @@
 def stencil(probes, coupling):
     np_, nx, ny, nz = probes.shape
     planes = nx + 2
-    field = pltpu.VMEM((np_ * planes, ny + 16, nz), jnp.float32)
+    field = pltpu.VMEM((np_ * planes, ny + 2 * LEAD, nz), jnp.float32)
     face = pltpu.VMEM((2, 2, np_, nx, nz), jnp.float32)
     return pl.pallas_call(
         functools.partial(stencil_kernel, np_, nx, ny),
@@ -232,34 +241,191 @@
     )(probes, coupling)
 
 
+def sense_kernel(np_, nx, ny, total_y, field, cell, frac, noise, slot, out, data):
+    tx, ty = lax.axis_index("tx"), lax.axis_index("ty")
+    lines, lanes = cell.shape
+    bf16, f32 = jnp.bfloat16, jnp.float32
+
+    def dot(a, b, dims=((1,), (0,))):
+        return lax.dot_general(a, b, (dims, ((), ())), preferred_element_type=f32)
+
+    def split(x):
+        high = x.astype(bf16)
+        rest = x - high.astype(f32)
+        middle = rest.astype(bf16)
+        return high, middle, (rest - middle.astype(f32)).astype(bf16)
+
+    shift_z = 128 .bit_length() - 1
+    shift_x = shift_z + total_y.bit_length() - 1
+    place = cell[...]
+    local_x = lax.shift_right_logical(place, shift_x) - tx * nx
+    local_y = (lax.shift_right_logical(place, shift_z) & (total_y - 1)) - ty * ny
+    inside = (local_x >= 0) & (local_x < nx) & (local_y >= 0) & (local_y < ny)
+    ones = jnp.where(inside, 1.0, 0.0)
+    count = jnp.sum(ones).astype(jnp.int32)
+
+    def iota(shape, dim):
+        return lax.broadcasted_iota(jnp.int32, shape, dim)
+
+    upto = jnp.where(iota((lanes, lanes), 0) <= iota((lanes, lanes), 1), 1.0, 0.0).astype(bf16)
+    before = jnp.where(iota((lines, lines), 1) < iota((lines, lines), 0), 1.0, 0.0).astype(bf16)
+    marks = ones.astype(bf16)
+    within = dot(marks, upto)
+    totals = dot(marks, jnp.ones((lanes, lanes), bf16))
+    rank = dot(before, totals.astype(bf16)) + within - 1.0
+    rank = jnp.where(inside, rank, -1.0).astype(jnp.int32)
+
+    def as_float(x):
+        return jnp.where(inside, x, 0).astype(f32)
+
+    parts = [as_float(local_x), as_float(local_y), as_float(place & 127)]
+    parts += [lax.shift_right_logical(slot[...], shift_z).astype(f32), (slot[...] & 127).astype(f32)]
+    parts += [x.astype(f32) for x in split(frac[...])] + [x.astype(f32) for x in split(noise[...])]
+    for k, part in enumerate(parts):
+        data[pl.ds(k, lines, stride=16), :] = part
+    for k in range(len(parts), 16):
+        data[pl.ds(k, lines, stride=16), :] = jnp.zeros((lines, lanes), f32)
+
+    out[...] = jnp.zeros_like(out)
+    row_id = iota((CHUNK, lanes), 0)
+    lane_id = iota((CHUNK, lanes), 1)
+
+    def chunk(n, _):
+        first = n * CHUNK
+        picked = jnp.zeros((CHUNK, 16), f32)
+        for r in range(lines):
+            hot = jnp.where(rank[r : r + 1, :] - first == row_id, 1.0, 0.0).astype(bf16)
+            picked = picked + dot(hot, data[pl.ds(16 * r, 16), :].astype(bf16), ((1,), (1,)))
+
+        def column(k):
+            return picked[:, k : k + 1]
+
+        line = (column(0) * ny + column(1)).astype(jnp.int32)
+        height = column(2).astype(jnp.int32)
+        high = column(3).astype(jnp.int32)
+        low = column(4).astype(jnp.int32)
+        part_up = column(5) + column(6) + column(7)
+        variance = column(8) + column(9) + column(10)
+        got = jnp.zeros((CHUNK, np_ * 128), f32)
+        wide = 128
+        for b in range(nx * ny // wide):
+            hot = jnp.where(line - b * wide == lane_id, 1.0, 0.0).astype(bf16)
+            for piece in split(field[pl.ds(b * wide, wide), :]):
+                got = got + dot(hot, piece)
+        weight = jnp.where(lane_id == height, 1.0 - part_up, 0.0) + jnp.where(lane_id == height + 1, part_up, 0.0)
+        energy = jnp.zeros((CHUNK, 1), f32)
+        for p in range(np_):
+            value = jnp.sum(got[:, p * 128 : (p + 1) * 128] * weight, axis=1, keepdims=True)
+            energy = energy + value * value
+        valid = row_id[:, :1] + first < count
+        grad = jnp.where(valid, -energy / jnp.where(valid, variance, 1.0), 0.0)
+        to_line = jnp.where(iota((CHUNK, lines), 1) == high, 1.0, 0.0)
+        to_lane = jnp.where(lane_id == low, grad, 0.0)
+        out[...] += lax.dot_general(
+            to_line, to_lane, (((0,), (0,)), ((), ())), precision=lax.Precision.HIGHEST, preferred_element_type=f32
+        )
+        return 0
+
+    lax.fori_loop(0, (count + CHUNK - 1) // CHUNK, chunk, 0)
+
+
+def sense(field, cell, frac, noise, slot, np_, nx, ny, total_y):
+    return pl.pallas_call(
+        functools.partial(sense_kernel, np_, nx, ny, total_y),
+        out_shape=jax.ShapeDtypeStruct(cell.shape, jnp.float32),
+        in_specs=[pl.BlockSpec(memory_space=pltpu.VMEM)] * 5,
+        out_specs=pl.BlockSpec(memory_space=pltpu.VMEM),
+        scratch_shapes=[pltpu.VMEM((16 * cell.shape[0], cell.shape[1]), jnp.float32)],
+        compiler_params=pltpu.CompilerParams(vmem_limit_bytes=32 << 20),
+        name="sense",
+    )(field, cell, frac, noise, slot)
+
+
+def collect_kernel(terms, out, first, rows, second, send1, recv1, send2, recv2):
+    me, tx, ty = lax.axis_index("probe"), lax.axis_index("tx"), lax.axis_index("ty")
+    n, ntx, nty = lax.axis_size("probe"), lax.axis_size("tx"), lax.axis_size("ty")
+    probes = [{"probe": lax.rem(me + k, n)} for k in range(n)]
+    pairs = [(a, b) for a in range(ntx) for b in range(nty)][1:]
+
+    def tile(a, b):
+        return {"tx": lax.rem(tx + a, ntx), "ty": lax.rem(ty + b, nty)}
+
+    barrier = pltpu.get_barrier_semaphore()
+    for k in range(1, n):
+        pl.semaphore_signal(barrier, inc=1, device_id=probes[k], device_id_type=MESH)
+    for a, b in pairs:
+        pl.semaphore_signal(barrier, inc=1, device_id=tile(a, b), device_id_type=MESH)
+    pl.semaphore_wait(barrier, n - 1 + len(pairs))
+
+    copies = []
+    for k in range(1, n):
+        cp = pltpu.make_async_remote_copy(
+            src_ref=terms.at[pl.ds(pl.multiple_of(lax.rem(me + k, n) * ntx, 8), ntx)],
+            dst_ref=first.at[k],
+            send_sem=send1.at[k],
+            recv_sem=recv1.at[k],
+            device_id=probes[k],
+            device_id_type=MESH,
+        )
+        cp.start()
+        copies.append(cp)
+    total = terms[pl.ds(pl.multiple_of(me * ntx, 8), ntx), :]
+    for k in range(1, n):
+        copies[k - 1].wait_recv()
+        total = total + first[k]
+    for a in range(ntx):
+        rows[a] = total[a : a + 1, :]
+    for a, b in pairs:
+        cp = pltpu.make_async_remote_copy(
+            src_ref=rows.at[lax.rem(tx + a, ntx)],
+            dst_ref=second.at[a * nty + b],
+            send_sem=send2.at[a * nty + b],
+            recv_sem=recv2.at[a * nty + b],
+            device_id=tile(a, b),
+            device_id_type=MESH,
+        )
+        cp.start()
+        copies.append(cp)
+    mine = rows[tx]
+    for cp, (a, b) in zip(copies[n - 1 :], pairs):
+        cp.wait_recv()
+        mine = mine + second[a * nty + b]
+    width = 128 // nty
+    result = mine
+    for b in range(1, nty):
+        result = jnp.where(ty == b, pltpu.roll(mine, 128 - width * b, 1), result)
+    out[...] = result[:, :width]
+    for cp in copies:
+        cp.wait_send()
+
+
+def collect(terms):
+    n, ntx, nty = lax.axis_size("probe"), lax.axis_size("tx"), lax.axis_size("ty")
+    return pl.pallas_call(
+        collect_kernel,
+        out_shape=jax.ShapeDtypeStruct((1, 128 // nty), jnp.float32),
+        in_specs=[pl.BlockSpec(memory_space=pltpu.VMEM)],
+        out_specs=pl.BlockSpec(memory_space=pltpu.VMEM),
+        scratch_shapes=[
+            pltpu.VMEM((n, ntx, 128), jnp.float32),
+            pltpu.VMEM((ntx, 1, 128), jnp.float32),
+            pltpu.VMEM((ntx * nty, 1, 128), jnp.float32),
+            pltpu.SemaphoreType.DMA((n,)),
+            pltpu.SemaphoreType.DMA((n,)),
+            pltpu.SemaphoreType.DMA((ntx * nty,)),
+            pltpu.SemaphoreType.DMA((ntx * nty,)),
+        ],
+        compiler_params=pltpu.CompilerParams(collective_id=1, has_side_effects=True),
+        name="collect",
+    )(terms)
+
+
 def shards(probes, coupling, sensor_cell, sensor_frac, noise_var, owner_slot):
-    cells_x = probes.shape[1]
-    cells_y = probes.shape[2]
-    depth_cells = probes.shape[3]
-    tile_x = lax.axis_index("tx")
-    tile_y = lax.axis_index("ty")
-    total_y = cells_y * lax.axis_size("ty")
-    tracer = stencil(probes, coupling)
-    plane_cells = total_y * depth_cells
-    global_x = sensor_cell // plane_cells
-    global_y = sensor_cell // depth_cells % total_y
-    global_z = sensor_cell % depth_cells
-    local_x = global_x - tile_x * cells_x
-    local_y = global_y - tile_y * cells_y
-    inside = (local_x >= 0) & (local_x < cells_x) & (local_y >= 0) & (local_y < cells_y)
-    line_index = jnp.clip(local_x, 0, cells_x - 1) * cells_y + jnp.clip(local_y, 0, cells_y - 1)
-    lines = tracer.reshape(cells_x * cells_y, 4, depth_cells)
-    picked = jnp.take(lines, line_index, axis=0)
-    heights = jnp.arange(depth_cells, dtype=jnp.int32)[None, :]
-    below_pick = (heights == global_z[:, None]).astype(jnp.float32)
-    above_pick = (heights == global_z[:, None] + 1).astype(jnp.float32)
-    below_value = jnp.sum(picked * below_pick[:, None], axis=2)
-    above_value = jnp.sum(picked * above_pick[:, None], axis=2)
-    values = (1.0 - sensor_frac)[:, None] * below_value + sensor_frac[:, None] * above_value
-    energy = jnp.sum(values * values, axis=1)
-    contrib = jnp.where(inside, -energy / noise_var, 0.0)
-    ordered = jnp.zeros_like(contrib).at[owner_slot].set(contrib)
-    return lax.psum_scatter(ordered, ("probe", "tx", "ty"), scatter_dimension=0, tiled=True)
+    np_, nx, ny, nz = probes.shape
+    field = stencil(probes, coupling).reshape(nx * ny, np_ * nz)
+    small = [a.reshape(-1, 128) for a in (sensor_cell, sensor_frac, noise_var, owner_slot)]
+    terms = sense(field, *small, np_, nx, ny, ny * lax.axis_size("ty"))
+    return collect(terms).reshape(-1)
 
 
 def solution(mesh):

time: 298 us -> 99.3 us (0.33)
  other arithmetic: 71.7 us -> 0 us
  blocking collectives: 65.1 us -> 0 us
  local copies, waits for them, and re-layouts: 54.4 us -> 5.36 us
  Pallas kernels: 107 us -> 93.7 us
    reduce_sum x2 -> x0, other arithmetic: 66.6 us -> none  [the longest x1 66.6 us: shards(): below_value = jnp.sum(picked * below_pick[:, None], axis=2)]
    unnamed x1 -> x0, blocking collectives: 65.1 us -> none
    pallas_call x1, Pallas kernels: 107 us -> 74.1 us  [stencil(): pl.pallas_call(functools.partial(stencil_kernel, np_, nx, ny), out_shape=...]
    gather x1 -> x0, local copies, waits for them, and re-layouts: 31.9 us -> none  [shards(): picked = jnp.take(lines, line_index, axis=0)]
    pallas_call x0 -> x2, Pallas kernels: none -> 19.6 us  [the longest x1 14.3 us: collect(): pl.pallas_call(collect_kernel, out_shape=jax.ShapeDtypeStruct((1, 128 //...]
    scatter x1 -> x0, local copies, waits for them, and re-layouts: 15.5 us -> none  [shards(): ordered = jnp.zeros_like(contrib).at[owner_slot].set(contrib)]
    convert_element_type x1 -> x0, other arithmetic: 4.21 us -> none  [shards(): below_pick = (heights == global_z[:, None]).astype(jnp.float32)]
    unnamed x17 -> x15, local copies, waits for them, and re-layouts: 2.2 us -> 5.36 us
where the time goes in v2:
time: 99.3 us; the launch traced here: 99.1 us
  Pallas kernels  93.7 us (94%)
  local copies, waits for them, and re-layouts  5.36 us (5%)
    pallas_call x1, Pallas kernels, stencil(): pl.pallas_call(functools.partial(stencil_kernel, np_, nx, ny), out_shape=...  74.1 us
    pallas_call x1, Pallas kernels, collect(): pl.pallas_call(collect_kernel, out_shape=jax.ShapeDtypeStruct((1, 128 //...  14.3 us
    unnamed x15, local copies, waits for them, and re-layouts  5.36 us
    pallas_call x1, Pallas kernels, sense(): pl.pallas_call(functools.partial(sense_kernel, np_, nx, ny, total_y), out...  5.26 us

profile of v2, /device:TPU:1, one launch (start us, length us, event | category | flops | bytes accessed | tf_op | source)
XLA Modules:
  0.0 99.1 jit_solution(11746828321480231796)
XLA Ops:
  0.0 0.0 copy-start
  0.0 2.0 %copy-done = f32[7,32,32,128]{3,2,1,0:T(8,128)S(1)} copy-done((f32[7,32,32,128]{3,2,1,0:T(8,128)S(1)}, f32[7,32,32,128]{3,2,1,0:T(8,128)}, u32[]{:S(2)}) %copy-start) | copy-done | bytes 3670040
  2.0 0.0 copy-start.1
  2.0 1.6 %copy-done.1 = f32[4,32,32,128]{3,2,1,0:T(8,128)S(1)} copy-done((f32[4,32,32,128]{3,2,1,0:T(8,128)S(1)}, f32[4,32,32,128]{3,2,1,0:T(8,128)}, u32[]{:S(2)}) %copy-start.1) | copy-done | bytes 2097176
  3.6 0.0 copy-start.3
  3.6 0.0 copy-start.4
  3.6 0.0 copy-start.5
  3.6 0.0 copy-start.6
  3.6 74.1 %stencil.1 = f32[32,32,512]{2,1,0:T(8,128)S(1)} custom-call(f32[4,32,32,128]{3,2,1,0:T(8,128)S(1)} %copy-done.1, f32[7,32,32,128]{3,2,1,0:T(8,128)S(1)} %copy-done), custom_call_target="tpu_custom_call" | custom-call | tf_op jit(solution)/shard_map/stencil/pallas_call | solution.py:223
  77.7 0.0 copy-done.3
  77.8 0.0 copy-done.4
  77.8 0.0 copy-done.5
  77.8 0.0 copy-done.6
  77.8 5.3 %sense.1.terms = f32[32,128]{1,0:T(8,128)S(1)} custom-call(f32[1024,512]{1,0:T(8,128)S(1)} %bitcast.6, s32[32,128]{1,0:T(8,128)S(1)} %bitcast.7, f32[32,128]{1,0:T(8,128)S(1)} %bitcast.8, f32[32,128]{1,0:T(8,128)S(1)} %bitcast.9, s32[32,128]{1,0:T(8,128)S(1)} %bitcast.10), custom_call_target="tpu_custom_call" | custom-call | tf_op jit(solution)/shard_map/sense/pallas_call | solution.py:333
  83.0 0.0 copy-start.2
  83.0 0.6 copy-done.2
  83.7 14.3 %collect.1 = f32[1,32]{1,0:T(1,128)} custom-call(f32[32,128]{1,0:T(8,128)} %copy-done.2), custom_call_target="tpu_custom_call" | custom-call | tf_op jit(solution)/shard_map/collect/pallas_call | solution.py:404
  98.0 1.1 %copy.8 = f32[32]{0:T(128)} copy(f32[32]{0:T(128)} %bitcast.11) | data formatting | bytes 256
Async XLA Ops:
  0.0 2.0 %copy-start = (f32[7,32,32,128]{3,2,1,0:T(8,128)S(1)}, f32[7,32,32,128]{3,2,1,0:T(8,128)}, u32[]{:S(2)}) copy-start(f32[7,32,32,128]{3,2,1,0:T(8,128)} %coup_hbm.1) | copy-start | bytes 11010052
  2.0 1.6 %copy-start.1 = (f32[4,32,32,128]{3,2,1,0:T(8,128)S(1)}, f32[4,32,32,128]{3,2,1,0:T(8,128)}, u32[]{:S(2)}) copy-start(f32[4,32,32,128]{3,2,1,0:T(8,128)} %probes_hbm.1) | copy-start | bytes 6291460
  3.6 74.1 %copy-start.3 = (s32[4096]{0:T(1024)S(1)}, s32[4096]{0:T(1024)}, u32[]{:S(2)}) copy-start(s32[4096]{0:T(1024)} %param.8) | copy-start | bytes 49156
  3.6 74.1 %copy-start.4 = (f32[4096]{0:T(1024)S(1)}, f32[4096]{0:T(1024)}, u32[]{:S(2)}) copy-start(f32[4096]{0:T(1024)} %param.9) | copy-start | bytes 49156
  3.6 74.1 %copy-start.5 = (f32[4096]{0:T(1024)S(1)}, f32[4096]{0:T(1024)}, u32[]{:S(2)}) copy-start(f32[4096]{0:T(1024)} %param.10) | copy-start | bytes 49156
  3.6 74.1 %copy-start.6 = (s32[4096]{0:T(1024)S(1)}, s32[4096]{0:T(1024)}, u32[]{:S(2)}) copy-start(s32[4096]{0:T(1024)} %param.11) | copy-start | bytes 49156
  83.0 0.6 copy-start.2

commit v3 on v2

--- a/solution.py
+++ b/solution.py
@@ -9,232 +9,304 @@
 
 STEPS = 16
 MESH = pl.DeviceIdType.MESH
-GROUP = 2
 LEAD = 8
-UNROLL = 4
+UNROLL_A = 17
+UNROLL_B = 16
 CHUNK = 320
 
 
+DIRECTIONS = ((-1, 0), (1, 0), (0, -1), (0, 1), (-1, -1), (-1, 1), (1, -1), (1, 1))
+X_DIRS, Y_DIRS, CORNERS = (0, 1), (2, 3), (4, 5, 6, 7)
+
+
 def stencil_kernel(
-    np_, nx, ny, probes_hbm, coup_hbm, out_hbm, va, vb, c, ysend, yrecv, load_sem, coup_sem, send_sem, recv_sem
+    np_, nx, ny, probes_hbm, coup_hbm, out_hbm,
+    va, vb, c, cyrecv, cysend, xrecv, yrecv, krecv, ysend, ksend,
+    load_sem, coup_sem, send_sem, recv_sem, csend_sem, crecv_sem,
 ):
-    planes = nx + 2
+    planes = nx + 4
     rows = ny + 2 * LEAD
-    bufs = (va, vb)
-    flat = tuple(v.reshape(np_ * planes * rows, 128) for v in bufs)
+    blocks = STEPS // 2
+    fa, fb = (v.reshape(np_ * planes * rows, 128) for v in (va, vb))
+    fc = c.reshape(7 * (nx + 2) * ny, 128)
     tx, ty = lax.axis_index("tx"), lax.axis_index("ty")
     ntx, nty = lax.axis_size("tx"), lax.axis_size("ty")
-    has = (tx > 0, tx < ntx - 1, ty > 0, ty < nty - 1)
-    where = ({"tx": tx - 1}, {"tx": tx + 1}, {"ty": ty - 1}, {"ty": ty + 1})
-
-    loads = []
+
+    def exists(sx, sy):
+        return (tx + sx >= 0) & (tx + sx < ntx) & (ty + sy >= 0) & (ty + sy < nty)
+
+    to = [exists(sx, sy) for sx, sy in DIRECTIONS]
+    from_ = [exists(-sx, -sy) for sx, sy in DIRECTIONS]
+    where = [{"tx": tx + sx, "ty": ty + sy} for sx, sy in DIRECTIONS]
+
+    def load(p):
+        return pltpu.make_async_copy(
+            probes_hbm.at[p], va.at[pl.ds(p * planes + 2, nx), pl.ds(LEAD, ny)], load_sem.at[p]
+        )
+
+    def load_coupling(k):
+        return pltpu.make_async_copy(coup_hbm.at[k], c.at[k, pl.ds(1, nx)], coup_sem.at[k])
+
+    load(0).start()
+    for k in range(7):
+        load_coupling(k).start()
+    for p in range(1, np_):
+        load(p).start()
+
+    tile = jnp.zeros((8, 128), jnp.float32)
+
+    def zero_field(q, _):
+        va[q, pl.ds(0, 8)] = tile
+        va[q, pl.ds(LEAD + ny, 8)] = tile
+        return 0
+
+    lax.fori_loop(0, np_ * planes, zero_field, 0)
     for p in range(np_):
-        cp = pltpu.make_async_copy(
-            probes_hbm.at[p], va.at[pl.ds(p * planes + 1, nx), pl.ds(LEAD, ny)], load_sem.at[p]
-        )
-        cp.start()
-        loads.append(cp)
-    cload = []
+        for q in (0, 1, nx + 2, nx + 3):
+            for t in range(ny // 8):
+                va[p * planes + q, pl.ds(LEAD + 8 * t, 8)] = tile
     for k in range(7):
-        cp = pltpu.make_async_copy(coup_hbm.at[k], c.at[k], coup_sem.at[k])
-        cp.start()
-        cload.append(cp)
-
-    zrow = jnp.zeros((8, 128), jnp.float32)
-    for buf in bufs:
-        for p in range(np_):
-            for q in (p * planes, p * planes + nx + 1):
-                for t in range(ny // 8):
-                    buf[q, pl.ds(LEAD + 8 * t, 8)] = zrow
-
-            def zero_rows(i, _, buf=buf, p=p):
-                buf[p * planes + 1 + i, pl.ds(0, 8)] = zrow
-                buf[p * planes + 1 + i, pl.ds(LEAD + ny, 8)] = zrow
-                return 0
-
-            lax.fori_loop(0, nx, zero_rows, 0)
+        for t in range(ny // 8):
+            for q in (0, nx + 1):
+                c[k, q, pl.ds(8 * t, 8)] = tile
+        for side in range(2):
+            for t in range(nx // 8):
+                cyrecv[side, k, pl.ds(8 * t, 8)] = tile
+    for par in range(2):
+        for side in range(2):
+            for p in range(np_):
+                for t in range(nx // 8):
+                    yrecv[par, side, p, 1, pl.ds(8 * t, 8)] = tile
 
     barrier = pltpu.get_barrier_semaphore()
-    for d in range(4):
-
-        @pl.when(has[d])
+    for d in range(8):
+
+        @pl.when(to[d])
         def _(d=d):
             pl.semaphore_signal(barrier, inc=1, device_id=where[d], device_id_type=MESH)
 
-    pl.semaphore_wait(barrier, sum(h.astype(jnp.int32) for h in has))
+    pl.semaphore_wait(barrier, sum(h.astype(jnp.int32) for h in to))
 
     def copy(d, par, p):
-        v = bufs[par]
-        if d < 2:
-            src = v.at[p * planes + (1 if d == 0 else nx), pl.ds(LEAD, ny)]
-            dst = v.at[p * planes + (nx + 1 if d == 0 else 0), pl.ds(LEAD, ny)]
+        if d in X_DIRS:
+            src = va.at[pl.ds(p * planes + (2 if d == 0 else nx), 2), pl.ds(LEAD, ny)]
+            dst = xrecv.at[par, d, p]
+        elif d in Y_DIRS:
+            src = ysend.at[d - 2, p]
+            dst = yrecv.at[par, d - 2, p]
         else:
-            src = ysend.at[par, d - 2, p]
-            dst = yrecv.at[par, d - 2, p]
+            src = ksend.at[d - 4, p]
+            dst = krecv.at[par, d - 4, p]
         return pltpu.make_async_remote_copy(
             src_ref=src,
             dst_ref=dst,
-            send_sem=send_sem.at[par, d, p],
+            send_sem=send_sem.at[d, p],
             recv_sem=recv_sem.at[par, d, p],
             device_id=where[d],
             device_id_type=MESH,
         )
 
-    opposite = (1, 0, 3, 2)
-
-    def face(par, p, row):
-        return flat[par], pl.ds((p * planes + 1) * rows + row, nx, stride=rows)
-
-    def pack(par, p):
-        for side, row in enumerate((LEAD, LEAD + ny - 1)):
-            ref, lines = face(par, p, row)
-            ysend[par, side, p] = ref[lines, :]
-
-    def send(par, p):
-        for d in (2, 3, 0, 1):
-
-            @pl.when(has[d])
+    def copy_coupling(d):
+        if d in X_DIRS:
+            src = c.at[:, 1 if d == 0 else nx]
+            dst = c.at[:, nx + 1 if d == 0 else 0]
+        else:
+            src, dst = cysend.at[d - 2], cyrecv.at[d - 2]
+        return pltpu.make_async_remote_copy(
+            src_ref=src,
+            dst_ref=dst,
+            send_sem=csend_sem.at[d],
+            recv_sem=crecv_sem.at[d],
+            device_id=where[d],
+            device_id_type=MESH,
+        )
+
+    def along_x(p, x, y, count):
+        return pl.ds((p * planes + x + 2) * rows + LEAD + y, count, stride=rows)
+
+    def start(dirs, par, p):
+        for d in dirs:
+
+            @pl.when(to[d])
             def _(d=d):
                 copy(d, par, p).start()
 
-    def wait_send(par, p):
-        for d in range(4):
-
-            @pl.when(has[d])
+    def pack_y(p):
+        for side, edge in enumerate(((0, 1), (ny - 1, ny - 2))):
+            for n, y in enumerate(edge):
+                ysend[side, p, n] = fa[along_x(p, 0, y, nx), :]
+        for d in CORNERS:
+            sx, sy = DIRECTIONS[d]
+            x, y = (0 if sx < 0 else nx - 1), (0 if sy < 0 else ny - 1)
+            ksend[d - 4, p] = va[p * planes + x + 2, pl.ds(LEAD + y, 1)]
+
+    def receive(par, p):
+        for d in (0, 1, 4, 5, 6, 7, 2, 3):
+
+            @pl.when(from_[d])
             def _(d=d):
-                copy(d, par, p).wait_send()
-
-    def receive(par, p):
-        for d in range(4):
-
-            @pl.when(has[opposite[d]])
+                sx, sy = DIRECTIONS[d]
+                x, y = (nx if sx < 0 else -1), (ny if sy < 0 else -1)
+                copy(d, par, p).wait_recv()
+                if d in X_DIRS:
+                    for n in range(2):
+                        q = p * planes + (nx + 2 if d == 0 else 0) + n
+                        va[q, pl.ds(LEAD, ny)] = xrecv[par, d, p, n]
+                elif d in Y_DIRS:
+                    fa[along_x(p, 0, y, nx), :] = yrecv[par, d - 2, p, 0]
+                else:
+                    va[p * planes + x + 2, pl.ds(LEAD + y, 1)] = krecv[par, d - 4, p]
+
+    def wait_sent(p):
+        for d in range(8):
+
+            @pl.when(to[d])
             def _(d=d):
-                copy(d, par, p).wait_recv()
-                if d >= 2:
-                    ref, at = face(par, p, LEAD + ny if d == 2 else LEAD - 1)
-                    ref[at, :] = yrecv[par, d - 2, p]
-
-    for p in range(np_):
-        loads[p].wait()
-        pack(0, p)
-        send(0, p)
+                copy(d, 0, p).wait_send()
+
+    def first_send(p):
+        load(p).wait()
+        pack_y(p)
+        start((2, 3, 4, 5, 6, 7, 0, 1), 0, p)
+
+    first_send(0)
     for k in range(7):
-        cload[k].wait()
+        load_coupling(k).wait()
     lane = lax.broadcasted_iota(jnp.int32, (8, 128), 1)
 
     def clip_edges(i, _):
         for t in range(ny // 8):
-            rows = pl.ds(8 * t, 8)
-            c[5, i, rows] = jnp.where(lane == 127, 0.0, c[5, i, rows])
-            c[6, i, rows] = jnp.where(lane == 0, 0.0, c[6, i, rows])
+            at = pl.ds(8 * t, 8)
+            c[5, i, at] = jnp.where(lane == 127, 0.0, c[5, i, at])
+            c[6, i, at] = jnp.where(lane == 0, 0.0, c[6, i, at])
         return 0
 
-    lax.fori_loop(0, nx, clip_edges, 0)
-
-    def compute(group, par):
-        src, dst = bufs[par], bufs[1 - par]
-        tiles = ny // 8
-
-        def at(p, plane, t, off=0):
-            return src[p * planes + plane, pl.ds(LEAD + 8 * t + off, 8)]
-
-        def one(i, prev, cur):
+    lax.fori_loop(1, nx + 1, clip_edges, 0)
+    for side, y in enumerate((0, ny - 1)):
+        for k in range(7):
+            cysend[side, k] = fc[pl.ds((k * (nx + 2) + 1) * ny + y, nx, stride=ny), :]
+    for d in (2, 3, 0, 1):
+
+        @pl.when(to[d])
+        def _(d=d):
+            copy_coupling(d).start()
+
+    for p in range(1, np_):
+        first_send(p)
+    for d in (0, 1, 2, 3):
+
+        @pl.when(from_[d])
+        def _(d=d):
+            copy_coupling(d).wait_recv()
+
+    def combine(coef, v, ahead, behind, up, down):
+        r = coef[0] * v
+        r = r + (coef[1] * ahead + coef[2] * behind)
+        r = r + (coef[3] * up + coef[4] * down)
+        return r + (coef[5] * pltpu.roll(v, 127, 1) + coef[6] * pltpu.roll(v, 1, 1))
+
+    def sweep(src, dst, p, first, count, tiles, unroll):
+        def at(x, t, off=0):
+            return src[p * planes + x + 2, pl.ds(LEAD + 8 * t + off, 8)]
+
+        def one(x, prev, cur):
             nxt = []
-            for t in range(tiles):
-                coef = [c[k, i, pl.ds(8 * t, 8)] for k in range(7)]
-                for g, p in enumerate(group):
-                    n = t * len(group) + g
-                    v = cur[n]
-                    ahead = at(p, i + 2, t)
-                    up = at(p, i + 1, t, 1)
-                    down = at(p, i + 1, t, -1)
-                    r = coef[0] * v
-                    r = r + (coef[1] * ahead + coef[2] * prev[n])
-                    r = r + (coef[3] * up + coef[4] * down)
-                    r = r + (coef[5] * pltpu.roll(v, 127, 1) + coef[6] * pltpu.roll(v, 1, 1))
-                    dst[p * planes + i + 1, pl.ds(LEAD + 8 * t, 8)] = r
-                    nxt.append(ahead)
+            for n, t in enumerate(tiles):
+                coef = [c[k, x + 1, pl.ds(8 * t, 8)] for k in range(7)]
+                ahead = at(x + 1, t)
+                dst[p * planes + x + 2, pl.ds(LEAD + 8 * t, 8)] = combine(
+                    coef, cur[n], ahead, prev[n], at(x, t, 1), at(x, t, -1)
+                )
+                nxt.append(ahead)
             return cur, tuple(nxt)
 
         def body(block, carry):
-            for u in range(UNROLL):
-                carry = one(block * UNROLL + u, *carry)
+            for u in range(unroll):
+                carry = one(first + block * unroll + u, *carry)
             return carry
 
-        order = [(t, p) for t in range(tiles) for p in group]
-        prev = tuple(at(p, 0, t) for t, p in order)
-        cur = tuple(at(p, 1, t) for t, p in order)
-        lax.fori_loop(0, nx // UNROLL, body, (prev, cur))
-
-    groups = [tuple(range(g, g + GROUP)) for g in range(0, np_, GROUP)]
-
-    def two_steps(it, _):
-        for par in range(2):
-            for group in groups:
-                for p in group:
-                    receive(par, p)
-                if par == 1:
-                    for p in group:
-                        wait_send(1 - par, p)
-                else:
-
-                    @pl.when(it > 0)
-                    def _():
-                        for p in group:
-                            wait_send(1 - par, p)
-
-                compute(group, par)
-                if par == 0:
-                    for p in group:
-                        pack(1 - par, p)
-                        send(1 - par, p)
-                else:
-
-                    @pl.when(it < STEPS // 2 - 1)
-                    def _():
-                        for p in group:
-                            pack(1 - par, p)
-                            send(1 - par, p)
+        init = tuple(at(first - 1, t) for t in tiles), tuple(at(first, t) for t in tiles)
+        lax.fori_loop(0, count // unroll, body, init)
+
+    def outer_rows(par, p):
+        for side, y in enumerate((ny, -1)):
+            inner = along = None
+            for t in range(nx // 8):
+                coef = [cyrecv[side, k, pl.ds(8 * t, 8)] for k in range(7)]
+                v = fa[along_x(p, 8 * t, y, 8), :]
+                ahead = fa[along_x(p, 8 * t + 1, y, 8), :]
+                behind = fa[along_x(p, 8 * t - 1, y, 8), :]
+                inner = fa[along_x(p, 8 * t, ny - 1 if side == 0 else 0, 8), :]
+                outer = yrecv[par, side, p, 1, pl.ds(8 * t, 8)]
+                up, down = (outer, inner) if side == 0 else (inner, outer)
+                fb[along_x(p, 8 * t, y, 8), :] = combine(coef, v, ahead, behind, up, down)
+
+    def save(p):
+        return pltpu.make_async_copy(
+            va.at[pl.ds(p * planes + 2, nx), pl.ds(LEAD, ny)], out_hbm.at[:, :, pl.ds(p * 128, 128)], load_sem.at[p]
+        )
+
+    def work(n, _):
+        block, p = n // np_, lax.rem(n, np_)
+        par = lax.rem(block, 2)
+        receive(par, p)
+        sweep(va, vb, p, -1, nx + 2, (0, 1, 2, 3), UNROLL_A)
+        outer_rows(par, p)
+        wait_sent(p)
+        sweep(vb, va, p, 0, nx, (0, 3), UNROLL_B)
+
+        @pl.when(block < blocks - 1)
+        def _():
+            pack_y(p)
+            start((2, 3, 4, 5, 6, 7), 1 - par, p)
+
+        sweep(vb, va, p, 0, nx, (1, 2), UNROLL_B)
+
+        @pl.when(block < blocks - 1)
+        def _():
+            start((0, 1), 1 - par, p)
 
         return 0
 
-    lax.fori_loop(0, STEPS // 2, two_steps, 0)
+    lax.fori_loop(0, blocks * np_, work, 0)
     for p in range(np_):
-        wait_send(1, p)
-        cp = pltpu.make_async_copy(
-            va.at[pl.ds(p * planes + 1, nx), pl.ds(LEAD, ny)],
-            out_hbm.at[:, :, pl.ds(p * 128, 128)],
-            load_sem.at[p],
-        )
-        cp.start()
+        save(p).start()
+    for d in (0, 1, 2, 3):
+
+        @pl.when(to[d])
+        def _(d=d):
+            copy_coupling(d).wait_send()
+
     for p in range(np_):
-        pltpu.make_async_copy(
-            va.at[pl.ds(p * planes + 1, nx), pl.ds(LEAD, ny)],
-            out_hbm.at[:, :, pl.ds(p * 128, 128)],
-            load_sem.at[p],
-        ).wait()
+        save(p).wait()
 
 
 def stencil(probes, coupling):
     np_, nx, ny, nz = probes.shape
-    planes = nx + 2
-    field = pltpu.VMEM((np_ * planes, ny + 2 * LEAD, nz), jnp.float32)
-    face = pltpu.VMEM((2, 2, np_, nx, nz), jnp.float32)
+    f32 = jnp.float32
+    field = pltpu.VMEM((np_ * (nx + 4), ny + 2 * LEAD, nz), f32)
     return pl.pallas_call(
         functools.partial(stencil_kernel, np_, nx, ny),
-        out_shape=jax.ShapeDtypeStruct((nx, ny, np_ * nz), jnp.float32),
-        in_specs=[pl.BlockSpec(memory_space=pl.ANY)] * 2,
+        out_shape=jax.ShapeDtypeStruct((nx, ny, np_ * nz), f32),
+        in_specs=[pl.BlockSpec(memory_space=pltpu.HBM)] * 2,
         out_specs=pl.BlockSpec(memory_space=pl.ANY),
         scratch_shapes=[
             field,
             field,
-            pltpu.VMEM(coupling.shape, jnp.float32),
-            face,
-            face,
+            pltpu.VMEM((7, nx + 2, ny, nz), f32),
+            pltpu.VMEM((2, 7, nx, nz), f32),
+            pltpu.VMEM((2, 7, nx, nz), f32),
+            pltpu.VMEM((2, 2, np_, 2, ny, nz), f32),
+            pltpu.VMEM((2, 2, np_, 2, nx, nz), f32),
+            pltpu.VMEM((2, 4, np_, 1, nz), f32),
+            pltpu.VMEM((2, np_, 2, nx, nz), f32),
+            pltpu.VMEM((4, np_, 1, nz), f32),
             pltpu.SemaphoreType.DMA((np_,)),
             pltpu.SemaphoreType.DMA((7,)),
-            pltpu.SemaphoreType.DMA((2, 4, np_)),
-            pltpu.SemaphoreType.DMA((2, 4, np_)),
+            pltpu.SemaphoreType.DMA((8, np_)),
+            pltpu.SemaphoreType.DMA((2, 8, np_)),
+            pltpu.SemaphoreType.DMA((4,)),
+            pltpu.SemaphoreType.DMA((4,)),
         ],
         compiler_params=pltpu.CompilerParams(collective_id=0, has_side_effects=True, vmem_limit_bytes=32 << 20),
         name="stencil",

time: 99.3 us -> 80.6 us (0.81)
  Pallas kernels: 93.7 us -> 74.9 us
    pallas_call x1, Pallas kernels: 74.1 us -> 54 us  [stencil(): pl.pallas_call(functools.partial(stencil_kernel, np_, nx, ny), out_shape=...]
    pallas_call x1, Pallas kernels: 14.3 us -> 15.7 us  [collect(): pl.pallas_call(collect_kernel, out_shape=jax.ShapeDtypeStruct((1, 128 //...]
where the time goes in v3:
time: 80.6 us; the launch traced here: 80.4 us
  Pallas kernels  74.9 us (93%)
  local copies, waits for them, and re-layouts  5.36 us (7%)
    pallas_call x1, Pallas kernels, stencil(): pl.pallas_call(functools.partial(stencil_kernel, np_, nx, ny), out_shape=...  54 us
    pallas_call x1, Pallas kernels, collect(): pl.pallas_call(collect_kernel, out_shape=jax.ShapeDtypeStruct((1, 128 //...  15.7 us
    unnamed x15, local copies, waits for them, and re-layouts  5.36 us
    pallas_call x1, Pallas kernels, sense(): pl.pallas_call(functools.partial(sense_kernel, np_, nx, ny, total_y), out...  5.26 us

profile of v3, /device:TPU:1, one launch (start us, length us, event | category | flops | bytes accessed | tf_op | source)
XLA Modules:
  0.0 80.4 jit_solution(13424526624316384570)
XLA Ops:
  0.0 0.0 copy-start
  0.0 2.0 %copy-done = f32[7,32,32,128]{3,2,1,0:T(8,128)S(1)} copy-done((f32[7,32,32,128]{3,2,1,0:T(8,128)S(1)}, f32[7,32,32,128]{3,2,1,0:T(8,128)}, u32[]{:S(2)}) %copy-start) | copy-done | bytes 3670040
  2.0 0.0 copy-start.1
  2.0 1.6 %copy-done.1 = f32[4,32,32,128]{3,2,1,0:T(8,128)S(1)} copy-done((f32[4,32,32,128]{3,2,1,0:T(8,128)S(1)}, f32[4,32,32,128]{3,2,1,0:T(8,128)}, u32[]{:S(2)}) %copy-start.1) | copy-done | bytes 2097176
  3.6 0.0 copy-start.3
  3.6 0.0 copy-start.4
  3.6 0.0 copy-start.5
  3.6 0.0 copy-start.6
  3.6 54.0 %stencil.1 = f32[32,32,512]{2,1,0:T(8,128)S(1)} custom-call(f32[4,32,32,128]{3,2,1,0:T(8,128)S(1)} %copy-done.1, f32[7,32,32,128]{3,2,1,0:T(8,128)S(1)} %copy-done), custom_call_target="tpu_custom_call" | custom-call | tf_op jit(solution)/shard_map/stencil/pallas_call | solution.py:288
  57.6 0.0 copy-done.3
  57.6 0.0 copy-done.4
  57.7 0.0 copy-done.5
  57.7 0.0 copy-done.6
  57.7 5.3 %sense.1.terms = f32[32,128]{1,0:T(8,128)S(1)} custom-call(f32[1024,512]{1,0:T(8,128)S(1)} %bitcast.6, s32[32,128]{1,0:T(8,128)S(1)} %bitcast.7, f32[32,128]{1,0:T(8,128)S(1)} %bitcast.8, f32[32,128]{1,0:T(8,128)S(1)} %bitcast.9, s32[32,128]{1,0:T(8,128)S(1)} %bitcast.10), custom_call_target="tpu_custom_call" | custom-call | tf_op jit(solution)/shard_map/sense/pallas_call | solution.py:405
  62.9 0.0 copy-start.2
  62.9 0.6 copy-done.2
  63.6 15.7 %collect.1 = f32[1,32]{1,0:T(1,128)} custom-call(f32[32,128]{1,0:T(8,128)} %copy-done.2), custom_call_target="tpu_custom_call" | custom-call | tf_op jit(solution)/shard_map/collect/pallas_call | solution.py:476
  79.2 1.1 %copy.8 = f32[32]{0:T(128)} copy(f32[32]{0:T(128)} %bitcast.11) | data formatting | bytes 256
Async XLA Ops:
  0.0 2.0 %copy-start = (f32[7,32,32,128]{3,2,1,0:T(8,128)S(1)}, f32[7,32,32,128]{3,2,1,0:T(8,128)}, u32[]{:S(2)}) copy-start(f32[7,32,32,128]{3,2,1,0:T(8,128)} %coup_hbm.1) | copy-start | bytes 11010052
  2.0 1.6 %copy-start.1 = (f32[4,32,32,128]{3,2,1,0:T(8,128)S(1)}, f32[4,32,32,128]{3,2,1,0:T(8,128)}, u32[]{:S(2)}) copy-start(f32[4,32,32,128]{3,2,1,0:T(8,128)} %probes_hbm.1) | copy-start | bytes 6291460
  3.6 54.0 %copy-start.3 = (s32[4096]{0:T(1024)S(1)}, s32[4096]{0:T(1024)}, u32[]{:S(2)}) copy-start(s32[4096]{0:T(1024)} %param.8) | copy-start | bytes 49156
  3.6 54.0 %copy-start.4 = (f32[4096]{0:T(1024)S(1)}, f32[4096]{0:T(1024)}, u32[]{:S(2)}) copy-start(f32[4096]{0:T(1024)} %param.9) | copy-start | bytes 49156
  3.6 54.0 %copy-start.5 = (f32[4096]{0:T(1024)S(1)}, f32[4096]{0:T(1024)}, u32[]{:S(2)}) copy-start(f32[4096]{0:T(1024)} %param.10) | copy-start | bytes 49156
  3.6 54.0 %copy-start.6 = (s32[4096]{0:T(1024)S(1)}, s32[4096]{0:T(1024)}, u32[]{:S(2)}) copy-start(s32[4096]{0:T(1024)} %param.11) | copy-start | bytes 49156
  62.9 0.6 copy-start.2

commit v4 on v3

--- a/solution.py
+++ b/solution.py
@@ -10,9 +10,7 @@
 STEPS = 16
 MESH = pl.DeviceIdType.MESH
 LEAD = 8
-UNROLL_A = 17
-UNROLL_B = 16
-CHUNK = 320
+CAPACITY = 288
 
 
 DIRECTIONS = ((-1, 0), (1, 0), (0, -1), (0, 1), (-1, -1), (-1, 1), (1, -1), (1, 1))
@@ -205,7 +203,7 @@
         r = r + (coef[3] * up + coef[4] * down)
         return r + (coef[5] * pltpu.roll(v, 127, 1) + coef[6] * pltpu.roll(v, 1, 1))
 
-    def sweep(src, dst, p, first, count, tiles, unroll):
+    def sweep(src, dst, p, first, count, tiles):
         def at(x, t, off=0):
             return src[p * planes + x + 2, pl.ds(LEAD + 8 * t + off, 8)]
 
@@ -220,13 +218,9 @@
                 nxt.append(ahead)
             return cur, tuple(nxt)
 
-        def body(block, carry):
-            for u in range(unroll):
-                carry = one(first + block * unroll + u, *carry)
-            return carry
-
-        init = tuple(at(first - 1, t) for t in tiles), tuple(at(first, t) for t in tiles)
-        lax.fori_loop(0, count // unroll, body, init)
+        carry = tuple(at(first - 1, t) for t in tiles), tuple(at(first, t) for t in tiles)
+        for x in range(first, first + count):
+            carry = one(x, *carry)
 
     def outer_rows(par, p):
         for side, y in enumerate((ny, -1)):
@@ -250,17 +244,17 @@
         block, p = n // np_, lax.rem(n, np_)
         par = lax.rem(block, 2)
         receive(par, p)
-        sweep(va, vb, p, -1, nx + 2, (0, 1, 2, 3), UNROLL_A)
+        sweep(va, vb, p, -1, nx + 2, (0, 1, 2, 3))
         outer_rows(par, p)
         wait_sent(p)
-        sweep(vb, va, p, 0, nx, (0, 3), UNROLL_B)
+        sweep(vb, va, p, 0, nx, (0, 3))
 
         @pl.when(block < blocks - 1)
         def _():
             pack_y(p)
             start((2, 3, 4, 5, 6, 7), 1 - par, p)
 
-        sweep(vb, va, p, 0, nx, (1, 2), UNROLL_B)
+        sweep(vb, va, p, 0, nx, (1, 2))
 
         @pl.when(block < blocks - 1)
         def _():
@@ -308,40 +302,55 @@
             pltpu.SemaphoreType.DMA((4,)),
             pltpu.SemaphoreType.DMA((4,)),
         ],
-        compiler_params=pltpu.CompilerParams(collective_id=0, has_side_effects=True, vmem_limit_bytes=32 << 20),
+        compiler_params=pltpu.CompilerParams(collective_id=0, has_side_effects=True, vmem_limit_bytes=56 << 20),
         name="stencil",
     )(probes, coupling)
 
 
-def sense_kernel(np_, nx, ny, total_y, field, cell, frac, noise, slot, out, data):
-    tx, ty = lax.axis_index("tx"), lax.axis_index("ty")
+def sensor_kernel(
+    np_, nx, ny, total_y, field, cell, frac, noise, slot,
+    out, crowded, data, terms, first, line_terms, second, send1, recv1, send2, recv2,
+):
+    me, tx, ty = lax.axis_index("probe"), lax.axis_index("tx"), lax.axis_index("ty")
+    n, ntx, nty = lax.axis_size("probe"), lax.axis_size("tx"), lax.axis_size("ty")
+    peers = [{"probe": lax.rem(me + k, n)} for k in range(n)]
+    pairs = [(a, b) for a in range(ntx) for b in range(nty)][1:]
+
+    def owner(a, b):
+        return {"tx": lax.rem(tx + a, ntx), "ty": lax.rem(ty + b, nty)}
+
+    barrier = pltpu.get_barrier_semaphore()
+    for k in range(1, n):
+        pl.semaphore_signal(barrier, inc=1, device_id=peers[k], device_id_type=MESH)
+    for a, b in pairs:
+        pl.semaphore_signal(barrier, inc=1, device_id=owner(a, b), device_id_type=MESH)
+
     lines, lanes = cell.shape
     bf16, f32 = jnp.bfloat16, jnp.float32
 
-    def dot(a, b, dims=((1,), (0,))):
-        return lax.dot_general(a, b, (dims, ((), ())), preferred_element_type=f32)
-
-    def split(x):
-        high = x.astype(bf16)
-        rest = x - high.astype(f32)
-        middle = rest.astype(bf16)
-        return high, middle, (rest - middle.astype(f32)).astype(bf16)
-
-    shift_z = 128 .bit_length() - 1
+    def dot(a, b, dims=((1,), (0,)), **kw):
+        return lax.dot_general(a, b, (dims, ((), ())), preferred_element_type=f32, **kw)
+
+    def split(x, count):
+        pieces = []
+        for _ in range(count):
+            pieces.append(x.astype(bf16))
+            x = x - pieces[-1].astype(f32)
+        return pieces
+
+    def iota(shape, dim):
+        return lax.broadcasted_iota(jnp.int32, shape, dim)
+
+    shift_z = lanes.bit_length() - 1
     shift_x = shift_z + total_y.bit_length() - 1
     place = cell[...]
-    local_x = lax.shift_right_logical(place, shift_x) - tx * nx
-    local_y = (lax.shift_right_logical(place, shift_z) & (total_y - 1)) - ty * ny
+    global_x = lax.shift_right_logical(place, shift_x)
+    global_y = lax.shift_right_logical(place, shift_z) & (total_y - 1)
+    local_x, local_y = global_x - tx * nx, global_y - ty * ny
     inside = (local_x >= 0) & (local_x < nx) & (local_y >= 0) & (local_y < ny)
-    ones = jnp.where(inside, 1.0, 0.0)
-    count = jnp.sum(ones).astype(jnp.int32)
-
-    def iota(shape, dim):
-        return lax.broadcasted_iota(jnp.int32, shape, dim)
-
+    marks = jnp.where(inside, 1.0, 0.0).astype(bf16)
     upto = jnp.where(iota((lanes, lanes), 0) <= iota((lanes, lanes), 1), 1.0, 0.0).astype(bf16)
     before = jnp.where(iota((lines, lines), 1) < iota((lines, lines), 0), 1.0, 0.0).astype(bf16)
-    marks = ones.astype(bf16)
     within = dot(marks, upto)
     totals = dot(marks, jnp.ones((lanes, lanes), bf16))
     rank = dot(before, totals.astype(bf16)) + within - 1.0
@@ -350,85 +359,39 @@
     def as_float(x):
         return jnp.where(inside, x, 0).astype(f32)
 
-    parts = [as_float(local_x), as_float(local_y), as_float(place & 127)]
-    parts += [lax.shift_right_logical(slot[...], shift_z).astype(f32), (slot[...] & 127).astype(f32)]
-    parts += [x.astype(f32) for x in split(frac[...])] + [x.astype(f32) for x in split(noise[...])]
-    for k, part in enumerate(parts):
-        data[pl.ds(k, lines, stride=16), :] = part
-    for k in range(len(parts), 16):
-        data[pl.ds(k, lines, stride=16), :] = jnp.zeros((lines, lanes), f32)
-
-    out[...] = jnp.zeros_like(out)
-    row_id = iota((CHUNK, lanes), 0)
-    lane_id = iota((CHUNK, lanes), 1)
-
-    def chunk(n, _):
-        first = n * CHUNK
-        picked = jnp.zeros((CHUNK, 16), f32)
-        for r in range(lines):
-            hot = jnp.where(rank[r : r + 1, :] - first == row_id, 1.0, 0.0).astype(bf16)
-            picked = picked + dot(hot, data[pl.ds(16 * r, 16), :].astype(bf16), ((1,), (1,)))
-
-        def column(k):
-            return picked[:, k : k + 1]
-
-        line = (column(0) * ny + column(1)).astype(jnp.int32)
-        height = column(2).astype(jnp.int32)
-        high = column(3).astype(jnp.int32)
-        low = column(4).astype(jnp.int32)
-        part_up = column(5) + column(6) + column(7)
-        variance = column(8) + column(9) + column(10)
-        got = jnp.zeros((CHUNK, np_ * 128), f32)
-        wide = 128
-        for b in range(nx * ny // wide):
-            hot = jnp.where(line - b * wide == lane_id, 1.0, 0.0).astype(bf16)
-            for piece in split(field[pl.ds(b * wide, wide), :]):
-                got = got + dot(hot, piece)
-        weight = jnp.where(lane_id == height, 1.0 - part_up, 0.0) + jnp.where(lane_id == height + 1, part_up, 0.0)
-        energy = jnp.zeros((CHUNK, 1), f32)
-        for p in range(np_):
-            value = jnp.sum(got[:, p * 128 : (p + 1) * 128] * weight, axis=1, keepdims=True)
-            energy = energy + value * value
-        valid = row_id[:, :1] + first < count
-        grad = jnp.where(valid, -energy / jnp.where(valid, variance, 1.0), 0.0)
-        to_line = jnp.where(iota((CHUNK, lines), 1) == high, 1.0, 0.0)
-        to_lane = jnp.where(lane_id == low, grad, 0.0)
-        out[...] += lax.dot_general(
-            to_line, to_lane, (((0,), (0,)), ((), ())), precision=lax.Precision.HIGHEST, preferred_element_type=f32
-        )
-        return 0
-
-    lax.fori_loop(0, (count + CHUNK - 1) // CHUNK, chunk, 0)
-
-
-def sense(field, cell, frac, noise, slot, np_, nx, ny, total_y):
-    return pl.pallas_call(
-        functools.partial(sense_kernel, np_, nx, ny, total_y),
-        out_shape=jax.ShapeDtypeStruct(cell.shape, jnp.float32),
-        in_specs=[pl.BlockSpec(memory_space=pltpu.VMEM)] * 5,
-        out_specs=pl.BlockSpec(memory_space=pltpu.VMEM),
-        scratch_shapes=[pltpu.VMEM((16 * cell.shape[0], cell.shape[1]), jnp.float32)],
-        compiler_params=pltpu.CompilerParams(vmem_limit_bytes=32 << 20),
-        name="sense",
-    )(field, cell, frac, noise, slot)
-
-
-def collect_kernel(terms, out, first, rows, second, send1, recv1, send2, recv2):
-    me, tx, ty = lax.axis_index("probe"), lax.axis_index("tx"), lax.axis_index("ty")
-    n, ntx, nty = lax.axis_size("probe"), lax.axis_size("tx"), lax.axis_size("ty")
-    probes = [{"probe": lax.rem(me + k, n)} for k in range(n)]
-    pairs = [(a, b) for a in range(ntx) for b in range(nty)][1:]
-
-    def tile(a, b):
-        return {"tx": lax.rem(tx + a, ntx), "ty": lax.rem(ty + b, nty)}
-
-    barrier = pltpu.get_barrier_semaphore()
-    for k in range(1, n):
-        pl.semaphore_signal(barrier, inc=1, device_id=probes[k], device_id_type=MESH)
-    for a, b in pairs:
-        pl.semaphore_signal(barrier, inc=1, device_id=tile(a, b), device_id_type=MESH)
+    parts = [as_float(local_x), as_float(local_y), as_float(place & (lanes - 1)), jnp.where(inside, 1.0, 0.0)]
+    parts += [lax.shift_right_logical(slot[...], shift_z).astype(f32), (slot[...] & (lanes - 1)).astype(f32)]
+    parts += [x.astype(f32) for x in split(frac[...], 3) + split(noise[...], 3)]
+    for k in range(16):
+        data[pl.ds(k, lines, stride=16), :] = parts[k] if k < len(parts) else jnp.zeros((lines, lanes), f32)
+
+    row_id = iota((CAPACITY, lanes), 0)
+    lane_id = iota((CAPACITY, lanes), 1)
+    picked = jnp.zeros((CAPACITY, 16), f32)
+    for r in range(lines):
+        hot = jnp.where(rank[r : r + 1, :] == row_id, 1.0, 0.0).astype(bf16)
+        picked = picked + dot(hot, data[pl.ds(16 * r, 16), :].astype(bf16), ((1,), (1,)))
+    local_x, local_y, height, valid, line, lane = (picked[:, k : k + 1].astype(jnp.int32) for k in range(6))
+    above = picked[:, 6:7] + picked[:, 7:8] + picked[:, 8:9]
+    variance = picked[:, 9:10] + picked[:, 10:11] + picked[:, 11:12]
+
+    got = jnp.zeros((CAPACITY, np_ * lanes), f32)
+    at = local_x * ny + local_y
+    for b in range(nx * ny // lanes):
+        hot = jnp.where(at - b * lanes == lane_id, 1.0, 0.0).astype(bf16)
+        for piece in split(field[pl.ds(b * lanes, lanes), :], 2):
+            got = got + dot(hot, piece)
+    weight = jnp.where(lane_id == height, 1.0 - above, 0.0) + jnp.where(lane_id == height + 1, above, 0.0)
+    energy = jnp.zeros((CAPACITY, 1), f32)
+    for p in range(np_):
+        value = jnp.sum(got[:, p * lanes : (p + 1) * lanes] * weight, axis=1, keepdims=True)
+        energy = energy + value * value
+    grad = jnp.where(valid > 0, -energy / jnp.where(valid > 0, variance, 1.0), 0.0)
+    to_line = jnp.where(iota((CAPACITY, lines), 1) == line, 1.0, 0.0)
+    to_lane = jnp.where(lane_id == lane, grad, 0.0)
+    terms[...] = dot(to_line, to_lane, ((0,), (0,)), precision=lax.Precision.HIGHEST)
+
     pl.semaphore_wait(barrier, n - 1 + len(pairs))
-
     copies = []
     for k in range(1, n):
         cp = pltpu.make_async_remote_copy(
@@ -436,68 +399,102 @@
             dst_ref=first.at[k],
             send_sem=send1.at[k],
             recv_sem=recv1.at[k],
-            device_id=probes[k],
+            device_id=peers[k],
             device_id_type=MESH,
         )
         cp.start()
         copies.append(cp)
+
+    region = lax.div(global_x, nx) * nty + lax.div(global_y, ny)
+    for r in range(ntx * nty):
+        data[r : r + 1, :] = jnp.sum(jnp.where(region == r, 1.0, 0.0), axis=0, keepdims=True)
+    most = jnp.max(jnp.sum(data[: ntx * nty, :], axis=1, keepdims=True))
+    crowded[0, 0] = (most > CAPACITY).astype(jnp.int32)
+
     total = terms[pl.ds(pl.multiple_of(me * ntx, 8), ntx), :]
     for k in range(1, n):
         copies[k - 1].wait_recv()
         total = total + first[k]
     for a in range(ntx):
-        rows[a] = total[a : a + 1, :]
+        line_terms[a] = total[a : a + 1, :]
     for a, b in pairs:
         cp = pltpu.make_async_remote_copy(
-            src_ref=rows.at[lax.rem(tx + a, ntx)],
+            src_ref=line_terms.at[lax.rem(tx + a, ntx)],
             dst_ref=second.at[a * nty + b],
             send_sem=send2.at[a * nty + b],
             recv_sem=recv2.at[a * nty + b],
-            device_id=tile(a, b),
+            device_id=owner(a, b),
             device_id_type=MESH,
         )
         cp.start()
         copies.append(cp)
-    mine = rows[tx]
+    mine = line_terms[tx]
     for cp, (a, b) in zip(copies[n - 1 :], pairs):
         cp.wait_recv()
         mine = mine + second[a * nty + b]
-    width = 128 // nty
+    width = lanes // nty
     result = mine
     for b in range(1, nty):
-        result = jnp.where(ty == b, pltpu.roll(mine, 128 - width * b, 1), result)
+        result = jnp.where(ty == b, pltpu.roll(mine, lanes - width * b, 1), result)
     out[...] = result[:, :width]
     for cp in copies:
         cp.wait_send()
 
 
-def collect(terms):
+def sensors(field, cell, frac, noise, slot, np_, nx, ny, total_y):
     n, ntx, nty = lax.axis_size("probe"), lax.axis_size("tx"), lax.axis_size("ty")
+    lines, lanes = cell.shape
+    f32 = jnp.float32
+    vmem = pl.BlockSpec(memory_space=pltpu.VMEM)
     return pl.pallas_call(
-        collect_kernel,
-        out_shape=jax.ShapeDtypeStruct((1, 128 // nty), jnp.float32),
-        in_specs=[pl.BlockSpec(memory_space=pltpu.VMEM)],
-        out_specs=pl.BlockSpec(memory_space=pltpu.VMEM),
+        functools.partial(sensor_kernel, np_, nx, ny, total_y),
+        out_shape=(jax.ShapeDtypeStruct((1, lanes // nty), f32), jax.ShapeDtypeStruct((1, 1), jnp.int32)),
+        in_specs=[vmem] * 5,
+        out_specs=(vmem, pl.BlockSpec(memory_space=pltpu.SMEM)),
         scratch_shapes=[
-            pltpu.VMEM((n, ntx, 128), jnp.float32),
-            pltpu.VMEM((ntx, 1, 128), jnp.float32),
-            pltpu.VMEM((ntx * nty, 1, 128), jnp.float32),
+            pltpu.VMEM((16 * lines, lanes), f32),
+            pltpu.VMEM((lines, lanes), f32),
+            pltpu.VMEM((n, ntx, lanes), f32),
+            pltpu.VMEM((ntx, 1, lanes), f32),
+            pltpu.VMEM((ntx * nty, 1, lanes), f32),
             pltpu.SemaphoreType.DMA((n,)),
             pltpu.SemaphoreType.DMA((n,)),
             pltpu.SemaphoreType.DMA((ntx * nty,)),
             pltpu.SemaphoreType.DMA((ntx * nty,)),
         ],
-        compiler_params=pltpu.CompilerParams(collective_id=1, has_side_effects=True),
-        name="collect",
-    )(terms)
+        compiler_params=pltpu.CompilerParams(collective_id=1, has_side_effects=True, vmem_limit_bytes=32 << 20),
+        name="sensors",
+    )(field, cell, frac, noise, slot)
+
+
+def sensors_of_any_number(field, cell, frac, noise, slot, np_, nx, ny, total_y):
+    cell, frac, noise, slot = (a.reshape(-1) for a in (cell, frac, noise, slot))
+    local_x = cell // (total_y * 128) - lax.axis_index("tx") * nx
+    local_y = cell // 128 % total_y - lax.axis_index("ty") * ny
+    height = cell % 128
+    inside = (local_x >= 0) & (local_x < nx) & (local_y >= 0) & (local_y < ny)
+    line = jnp.clip(local_x, 0, nx - 1) * ny + jnp.clip(local_y, 0, ny - 1)
+    picked = jnp.take(field, line, axis=0).reshape(-1, np_, 128)
+    heights = jnp.arange(128, dtype=jnp.int32)[None, :]
+    below = jnp.sum(jnp.where((heights == height[:, None])[:, None], picked, 0.0), axis=2)
+    above = jnp.sum(jnp.where((heights == height[:, None] + 1)[:, None], picked, 0.0), axis=2)
+    values = (1.0 - frac)[:, None] * below + frac[:, None] * above
+    terms = jnp.where(inside, -jnp.sum(values * values, axis=1) / noise, 0.0)
+    ordered = jnp.zeros_like(terms).at[slot].set(terms)
+    return lax.psum_scatter(ordered, ("probe", "tx", "ty"), scatter_dimension=0, tiled=True)
 
 
 def shards(probes, coupling, sensor_cell, sensor_frac, noise_var, owner_slot):
     np_, nx, ny, nz = probes.shape
     field = stencil(probes, coupling).reshape(nx * ny, np_ * nz)
     small = [a.reshape(-1, 128) for a in (sensor_cell, sensor_frac, noise_var, owner_slot)]
-    terms = sense(field, *small, np_, nx, ny, ny * lax.axis_size("ty"))
-    return collect(terms).reshape(-1)
+    sizes = (np_, nx, ny, ny * lax.axis_size("ty"))
+    gradient, crowded = sensors(field, *small, *sizes)
+    return lax.cond(
+        crowded[0, 0] > 0,
+        lambda: sensors_of_any_number(field, *small, *sizes),
+        lambda: gradient.reshape(-1),
+    )
 
 
 def solution(mesh):

time: 80.6 us -> 62.3 us (0.77)
  Pallas kernels: 74.9 us -> 60.9 us
  local copies, waits for them, and re-layouts: 5.36 us -> 0.53 us
    pallas_call x1, Pallas kernels: 54 us -> 44.8 us  [stencil(): pl.pallas_call(functools.partial(stencil_kernel, np_, nx, ny), out_shape=...]
    pallas_call x2 -> x1, Pallas kernels: 20.9 us -> 16.1 us  [sensors(): pl.pallas_call(functools.partial(sensor_kernel, np_, nx, ny, total_y), ou...]
    unnamed x15 -> x9, local copies, waits for them, and re-layouts: 5.36 us -> 0.53 us
where the time goes in v4:
time: 62.3 us; the launch traced here: 62.2 us
  Pallas kernels  60.9 us (98%)
  between operations  0.76 us (1%)
    pallas_call x1, Pallas kernels, stencil(): pl.pallas_call(functools.partial(stencil_kernel, np_, nx, ny), out_shape=...  44.8 us
    pallas_call x1, Pallas kernels, sensors(): pl.pallas_call(functools.partial(sensor_kernel, np_, nx, ny, total_y), ou...  16.1 us

profile of v4, /device:TPU:1, one launch (start us, length us, event | category | flops | bytes accessed | tf_op | source)
XLA Modules:
  0.0 62.2 jit_solution(18134878089082922990)
XLA Ops:
  0.0 0.0 copy-start
  0.0 0.0 copy-start.1
  0.0 0.0 copy-start.3
  0.0 0.0 copy-start.2
  0.0 44.8 %stencil.1 = f32[32,32,512]{2,1,0:T(8,128)S(1)} custom-call(f32[4,32,32,128]{3,2,1,0:T(8,128)} %probes_hbm.1, f32[7,32,32,128]{3,2,1,0:T(8,128)} %coup_hbm.1), custom_call_target="tpu_custom_call" | custom-call | tf_op jit(solution)/shard_map/stencil/pallas_call | solution.py:282
  44.8 0.0 copy-done
  44.8 0.0 copy-done.1
  44.9 0.0 copy-done.3
  44.9 0.0 copy-done.2
  44.9 16.1 %sensors.1 = (f32[1,32]{1,0:T(1,128)S(1)}, s32[1,1]{1,0:T(1,128)}) custom-call(f32[1024,512]{1,0:T(8,128)S(1)} %bitcast.7, s32[32,128]{1,0:T(8,128)S(1)} %bitcast.9, f32[32,128]{1,0:T(8,128)S(1)} %bitcast.10, f32[32,128]{1,0:T(8,128)S(1)} %bitcast.12, s32[32,128]{1,0:T(8,128)S(1)} %bitcast.11), custom_call_target="tpu_custom_call" | custom-call | tf_op jit(solution)/shard_map/sensors/pallas_call | solution.py:449
  61.6 0.5 copy.19
  (1 shorter events, 0.0 us)
Async XLA Ops:
  0.0 44.8 %copy-start = (s32[4096]{0:T(1024)S(1)}, s32[4096]{0:T(1024)}, u32[]{:S(2)}) copy-start(s32[4096]{0:T(1024)} %param.10) | copy-start | bytes 49156
  0.0 44.8 %copy-start.1 = (f32[4096]{0:T(1024)S(1)}, f32[4096]{0:T(1024)}, u32[]{:S(2)}) copy-start(f32[4096]{0:T(1024)} %param.11) | copy-start | bytes 49156
  0.0 44.9 %copy-start.3 = (f32[4096]{0:T(1024)S(1)}, f32[4096]{0:T(1024)}, u32[]{:S(2)}) copy-start(f32[4096]{0:T(1024)} %param.12) | copy-start | bytes 49156
  0.0 44.9 %copy-start.2 = (s32[4096]{0:T(1024)S(1)}, s32[4096]{0:T(1024)}, u32[]{:S(2)}) copy-start(s32[4096]{0:T(1024)} %param.13) | copy-start | bytes 49156

commit v5 on v4

v5 whole, which is shorter than its diff:
```python
import functools

import jax
import jax.numpy as jnp
from jax import lax
from jax.experimental import pallas as pl
from jax.experimental.pallas import tpu as pltpu
from jax.sharding import PartitionSpec as P

STEPS = 16
MESH = pl.DeviceIdType.MESH
LEAD = 8
CAPACITY = 288


DIRECTIONS = ((-1, 0), (1, 0), (0, -1), (0, 1), (-1, -1), (-1, 1), (1, -1), (1, 1))
X_DIRS, Y_DIRS, CORNERS = (0, 1), (2, 3), (4, 5, 6, 7)


def kernel(
    np_, nx, ny, probes_hbm, coup_hbm, cell, frac, noise, slot,
    out, crowded, out_hbm,
    va, vb, c, cyrecv, cysend, xrecv, yrecv, krecv, ysend, ksend, data, chosen, terms, gathered,
    load_sem, coup_sem, send_sem, recv_sem, csend_sem, crecv_sem, sum_send, sum_recv,
):
    planes = nx + 4
    rows = ny + 2 * LEAD
    blocks = STEPS // 2
    fa, fb = (v.reshape(np_ * planes * rows, 128) for v in (va, vb))
    fc = c.reshape(7 * (nx + 2) * ny, 128)
    me, tx, ty = lax.axis_index("probe"), lax.axis_index("tx"), lax.axis_index("ty")
    n_probe, ntx, nty = lax.axis_size("probe"), lax.axis_size("tx"), lax.axis_size("ty")

    def exists(sx, sy):
        return (tx + sx >= 0) & (tx + sx < ntx) & (ty + sy >= 0) & (ty + sy < nty)

    to = [exists(sx, sy) for sx, sy in DIRECTIONS]
    from_ = [exists(-sx, -sy) for sx, sy in DIRECTIONS]
    where = [{"tx": tx + sx, "ty": ty + sy} for sx, sy in DIRECTIONS]

    def load(p):
        return pltpu.make_async_copy(
            probes_hbm.at[p], va.at[pl.ds(p * planes + 2, nx), pl.ds(LEAD, ny)], load_sem.at[p]
        )

    def load_coupling(k):
        return pltpu.make_async_copy(coup_hbm.at[k], c.at[k, pl.ds(1, nx)], coup_sem.at[k])

    load(0).start()
    for k in range(7):
        load_coupling(k).start()
    for p in range(1, np_):
        load(p).start()

    tile = jnp.zeros((8, 128), jnp.float32)

    for k in range(7):
        for t in range(ny // 8):
            for q in (0, nx + 1):
                c[k, q, pl.ds(8 * t, 8)] = tile
        for side in range(2):
            for t in range(nx // 8):
                cyrecv[side, k, pl.ds(8 * t, 8)] = tile
    for par in range(2):
        for side in range(2):
            for p in range(np_):
                for t in range(nx // 8):
                    yrecv[par, side, p, 1, pl.ds(8 * t, 8)] = tile

    barrier = pltpu.get_barrier_semaphore()
    for d in range(8):

        @pl.when(to[d])
        def _(d=d):
            pl.semaphore_signal(barrier, inc=1, device_id=where[d], device_id_type=MESH)

    for k in range(1, n_probe):
        pl.semaphore_signal(barrier, inc=1, device_id={"probe": lax.rem(me + k, n_probe)}, device_id_type=MESH)

    def zero_field(q, _):
        va[q, pl.ds(0, 8)] = tile
        va[q, pl.ds(LEAD + ny, 8)] = tile
        return 0

    lax.fori_loop(0, np_ * planes, zero_field, 0)
    for p in range(np_):
        for q in (0, 1, nx + 2, nx + 3):
            for t in range(ny // 8):
                va[p * planes + q, pl.ds(LEAD + 8 * t, 8)] = tile
    choose_sensors(nx, ny, nty, ntx, tx, ty, cell, frac, noise, slot, crowded, data, chosen)
    pl.semaphore_wait(barrier, n_probe - 1 + sum(h.astype(jnp.int32) for h in to))

    def copy(d, par, p):
        if d in X_DIRS:
            src = va.at[pl.ds(p * planes + (2 if d == 0 else nx), 2), pl.ds(LEAD, ny)]
            dst = xrecv.at[par, d, p]
        elif d in Y_DIRS:
            src = ysend.at[d - 2, p]
            dst = yrecv.at[par, d - 2, p]
        else:
            src = ksend.at[d - 4, p]
            dst = krecv.at[par, d - 4, p]
        return pltpu.make_async_remote_copy(
            src_ref=src,
            dst_ref=dst,
            send_sem=send_sem.at[d, p],
            recv_sem=recv_sem.at[par, d, p],
            device_id=where[d],
            device_id_type=MESH,
        )

    def copy_coupling(d):
        if d in X_DIRS:
            src = c.at[:, 1 if d == 0 else nx]
            dst = c.at[:, nx + 1 if d == 0 else 0]
        else:
            src, dst = cysend.at[d - 2], cyrecv.at[d - 2]
        return pltpu.make_async_remote_copy(
            src_ref=src,
            dst_ref=dst,
            send_sem=csend_sem.at[d],
            recv_sem=crecv_sem.at[d],
            device_id=where[d],
            device_id_type=MESH,
        )

    def along_x(p, x, y, count):
        return pl.ds((p * planes + x + 2) * rows + LEAD + y, count, stride=rows)

    def start(dirs, par, p):
        for d in dirs:

            @pl.when(to[d])
            def _(d=d):
                copy(d, par, p).start()

    def pack_y(p):
        for side, edge in enumerate(((0, 1), (ny - 1, ny - 2))):
            for n, y in enumerate(edge):
                ysend[side, p, n] = fa[along_x(p, 0, y, nx), :]
        for d in CORNERS:
            sx, sy = DIRECTIONS[d]
            x, y = (0 if sx < 0 else nx - 1), (0 if sy < 0 else ny - 1)
            ksend[d - 4, p] = va[p * planes + x + 2, pl.ds(LEAD + y, 1)]

    def receive(par, p):
        for d in (0, 1, 4, 5, 6, 7, 2, 3):

            @pl.when(from_[d])
            def _(d=d):
                sx, sy = DIRECTIONS[d]
                x, y = (nx if sx < 0 else -1), (ny if sy < 0 else -1)
                copy(d, par, p).wait_recv()
                if d in X_DIRS:
                    for n in range(2):
                        q = p * planes + (nx + 2 if d == 0 else 0) + n
                        va[q, pl.ds(LEAD, ny)] = xrecv[par, d, p, n]
                elif d in Y_DIRS:
                    fa[along_x(p, 0, y, nx), :] = yrecv[par, d - 2, p, 0]
                else:
                    va[p * planes + x + 2, pl.ds(LEAD + y, 1)] = krecv[par, d - 4, p]

    def wait_sent(p):
        for d in range(8):

            @pl.when(to[d])
            def _(d=d):
                copy(d, 0, p).wait_send()

    def first_send(p):
        load(p).wait()
        pack_y(p)
        start((2, 3, 4, 5, 6, 7, 0, 1), 0, p)

    first_send(0)
    for k in range(7):
        load_coupling(k).wait()
    lane = lax.broadcasted_iota(jnp.int32, (8, 128), 1)

    def clip_edges(i, _):
        for t in range(ny // 8):
            at = pl.ds(8 * t, 8)
            c[5, i, at] = jnp.where(lane == 127, 0.0, c[5, i, at])
            c[6, i, at] = jnp.where(lane == 0, 0.0, c[6, i, at])
        return 0

    lax.fori_loop(1, nx + 1, clip_edges, 0)
    for side, y in enumerate((0, ny - 1)):
        for k in range(7):
            cysend[side, k] = fc[pl.ds((k * (nx + 2) + 1) * ny + y, nx, stride=ny), :]
    for d in (2, 3, 0, 1):

        @pl.when(to[d])
        def _(d=d):
            copy_coupling(d).start()

    for p in range(1, np_):
        first_send(p)
    for d in (0, 1, 2, 3):

        @pl.when(from_[d])
        def _(d=d):
            copy_coupling(d).wait_recv()

    def combine(coef, v, ahead, behind, up, down):
        r = coef[0] * v
        r = r + (coef[1] * ahead + coef[2] * behind)
        r = r + (coef[3] * up + coef[4] * down)
        return r + (coef[5] * pltpu.roll(v, 127, 1) + coef[6] * pltpu.roll(v, 1, 1))

    def sweep(src, dst, p, first, count, tiles):
        def at(x, t, off=0):
            return src[p * planes + x + 2, pl.ds(LEAD + 8 * t + off, 8)]

        def one(x, prev, cur):
            nxt = []
            for n, t in enumerate(tiles):
                coef = [c[k, x + 1, pl.ds(8 * t, 8)] for k in range(7)]
                ahead = at(x + 1, t)
                dst[p * planes + x + 2, pl.ds(LEAD + 8 * t, 8)] = combine(
                    coef, cur[n], ahead, prev[n], at(x, t, 1), at(x, t, -1)
                )
                nxt.append(ahead)
            return cur, tuple(nxt)

        carry = tuple(at(first - 1, t) for t in tiles), tuple(at(first, t) for t in tiles)
        for x in range(first, first + count):
            carry = one(x, *carry)

    def outer_rows(par, p):
        for side, y in enumerate((ny, -1)):
            inner = along = None
            for t in range(nx // 8):
                coef = [cyrecv[side, k, pl.ds(8 * t, 8)] for k in range(7)]
                v = fa[along_x(p, 8 * t, y, 8), :]
                ahead = fa[along_x(p, 8 * t + 1, y, 8), :]
                behind = fa[along_x(p, 8 * t - 1, y, 8), :]
                inner = fa[along_x(p, 8 * t, ny - 1 if side == 0 else 0, 8), :]
                outer = yrecv[par, side, p, 1, pl.ds(8 * t, 8)]
                up, down = (outer, inner) if side == 0 else (inner, outer)
                fb[along_x(p, 8 * t, y, 8), :] = combine(coef, v, ahead, behind, up, down)

    def save(p):
        return pltpu.make_async_copy(
            va.at[pl.ds(p * planes + 2, nx), pl.ds(LEAD, ny)], out_hbm.at[:, :, pl.ds(p * 128, 128)], load_sem.at[p]
        )

    def work(n, _):
        block, p = n // np_, lax.rem(n, np_)
        par = lax.rem(block, 2)
        receive(par, p)
        sweep(va, vb, p, -1, nx + 2, (0, 1, 2, 3))
        outer_rows(par, p)
        wait_sent(p)
        sweep(vb, va, p, 0, nx, (0, 3))

        @pl.when(block < blocks - 1)
        def _():
            pack_y(p)
            start((2, 3, 4, 5, 6, 7), 1 - par, p)

        sweep(vb, va, p, 0, nx, (1, 2))

        @pl.when(block < blocks - 1)
        def _():
            start((0, 1), 1 - par, p)

        @pl.when(block == blocks - 1)
        def _():
            save(p).start()

        return 0

    lax.fori_loop(0, blocks * np_, work, 0)

    sensor_terms(np_, nx, ny, planes, va, chosen, terms)
    offsets = [(k, a, b) for k in range(n_probe) for a in range(ntx) for b in range(nty)]
    place = {o: i for i, o in enumerate(offsets)}

    def far(o):
        k, a, b = o
        return min(k, n_probe - k) + min(a, ntx - a) / 2 + min(b, nty - b)

    for o in sorted(offsets[1:], key=far, reverse=True):
        k, a, b = o
        to_probe, to_tx, to_ty = lax.rem(me + k, n_probe), lax.rem(tx + a, ntx), lax.rem(ty + b, nty)
        pltpu.make_async_remote_copy(
            src_ref=terms.at[to_probe * ntx + to_tx],
            dst_ref=gathered.at[place[o]],
            send_sem=sum_send,
            recv_sem=sum_recv,
            device_id={"probe": to_probe, "tx": to_tx, "ty": to_ty},
            device_id_type=MESH,
        ).start()
    gathered[0] = terms[me * ntx + tx]
    for d in (0, 1, 2, 3):

        @pl.when(to[d])
        def _(d=d):
            copy_coupling(d).wait_send()

    for p in range(np_):
        save(p).wait()
    others = gathered.at[pl.ds(1, len(offsets) - 1)]
    every = pltpu.make_async_remote_copy(
        src_ref=others,
        dst_ref=others,
        send_sem=sum_send,
        recv_sem=sum_recv,
        device_id={"probe": lax.rem(me + 1, n_probe)},
        device_id_type=MESH,
    )
    every.wait_recv()
    sums = [gathered[i] for i in range(8)]
    for i in range(8, len(offsets)):
        sums[i % 8] = sums[i % 8] + gathered[i]
    while len(sums) > 1:
        sums = [u + v for u, v in zip(sums[::2], sums[1::2])]
    lanes = cell.shape[1]
    width = lanes // nty
    result = sums[0]
    for b in range(1, nty):
        result = jnp.where(ty == b, pltpu.roll(sums[0], lanes - width * b, 1), result)
    out[...] = result[:, :width]
    every.wait_send()


def dot(a, b, dims=((1,), (0,)), **kw):
    return lax.dot_general(a, b, (dims, ((), ())), preferred_element_type=jnp.float32, **kw)


def split(x, count):
    pieces = []
    for _ in range(count):
        pieces.append(x.astype(jnp.bfloat16))
        x = x - pieces[-1].astype(jnp.float32)
    return pieces


def iota(shape, dim):
    return lax.broadcasted_iota(jnp.int32, shape, dim)


def choose_sensors(nx, ny, nty, ntx, tx, ty, cell, frac, noise, slot, crowded, data, chosen):
    lines, lanes = cell.shape
    bf16, f32 = jnp.bfloat16, jnp.float32
    total_y = ny * nty
    shift_z = lanes.bit_length() - 1
    shift_x = shift_z + total_y.bit_length() - 1
    place = cell[...]
    global_x = lax.shift_right_logical(place, shift_x)
    global_y = lax.shift_right_logical(place, shift_z) & (total_y - 1)
    region = lax.div(global_x, nx) * nty + lax.div(global_y, ny)
    for r in range(ntx * nty):
        data[r : r + 1, :] = jnp.sum(jnp.where(region == r, 1.0, 0.0), axis=0, keepdims=True)
    most = jnp.max(jnp.sum(data[: ntx * nty, :], axis=1, keepdims=True))
    crowded[0, 0] = (most > CAPACITY).astype(jnp.int32)

    local_x, local_y = global_x - tx * nx, global_y - ty * ny
    inside = region == tx * nty + ty
    marks = jnp.where(inside, 1.0, 0.0).astype(bf16)
    upto = jnp.where(iota((lanes, lanes), 0) <= iota((lanes, lanes), 1), 1.0, 0.0).astype(bf16)
    before = jnp.where(iota((lines, lines), 1) < iota((lines, lines), 0), 1.0, 0.0).astype(bf16)
    within = dot(marks, upto)
    totals = dot(marks, jnp.ones((lanes, lanes), bf16))
    rank = dot(before, totals.astype(bf16)) + within - 1.0
    rank = jnp.where(inside, rank, -1.0).astype(jnp.int32)

    def as_float(x):
        return jnp.where(inside, x, 0).astype(f32)

    parts = [as_float(local_x), as_float(local_y), as_float(place & (lanes - 1)), jnp.where(inside, 1.0, 0.0)]
    parts += [lax.shift_right_logical(slot[...], shift_z).astype(f32), (slot[...] & (lanes - 1)).astype(f32)]
    parts += [x.astype(f32) for x in split(frac[...], 3) + split(noise[...], 3)]
    for k in range(16):
        data[pl.ds(k, lines, stride=16), :] = parts[k] if k < len(parts) else jnp.zeros((lines, lanes), f32)
    row_id = iota((CAPACITY, lanes), 0)
    picked = jnp.zeros((CAPACITY, 16), f32)
    for r in range(lines):
        hot = jnp.where(rank[r : r + 1, :] == row_id, 1.0, 0.0).astype(bf16)
        picked = picked + dot(hot, data[pl.ds(16 * r, 16), :].astype(bf16), ((1,), (1,)))
    chosen[...] = picked


def sensor_terms(np_, nx, ny, planes, field, chosen, terms):
    bf16, f32 = jnp.bfloat16, jnp.float32
    lines, _, lanes = terms.shape
    lane_id = iota((CAPACITY, lanes), 1)
    picked = chosen[...]
    local_x, local_y, height, valid, line, lane = (picked[:, k : k + 1].astype(jnp.int32) for k in range(6))
    above = picked[:, 6:7] + picked[:, 7:8] + picked[:, 8:9]
    variance = picked[:, 9:10] + picked[:, 10:11] + picked[:, 11:12]
    got = jnp.zeros((CAPACITY, np_ * lanes), f32)
    at = local_x * ny + local_y
    deep = 2 * lanes
    wide_id = iota((CAPACITY, deep), 1)
    for b in range(nx * ny // deep):
        hot = jnp.where(at - b * deep == wide_id, 1.0, 0.0).astype(bf16)
        count = deep // ny
        cells = [
            field[pl.ds(p * planes + 2 + b * count, count), pl.ds(LEAD, ny)].reshape(deep, lanes) for p in range(np_)
        ]
        for piece in split(jnp.concatenate(cells, axis=1), 2):
            got = got + dot(hot, piece)
    weight = jnp.where(lane_id == height, 1.0 - above, 0.0) + jnp.where(lane_id == height + 1, above, 0.0)
    energy = jnp.zeros((CAPACITY, 1), f32)
    for p in range(np_):
        value = jnp.sum(got[:, p * lanes : (p + 1) * lanes] * weight, axis=1, keepdims=True)
        energy = energy + value * value
    grad = jnp.where(valid > 0, -energy / jnp.where(valid > 0, variance, 1.0), 0.0)
    to_line = jnp.where(iota((CAPACITY, lines), 1) == line, 1.0, 0.0)
    to_lane = jnp.where(lane_id == lane, grad, 0.0)
    ordered = dot(to_line, to_lane, ((0,), (0,)), precision=lax.Precision.HIGHEST)
    for n in range(lines):
        terms[n] = ordered[n : n + 1, :]


def whole(probes, coupling, cell, frac, noise, slot):
    np_, nx, ny, nz = probes.shape
    f32 = jnp.float32
    lines, lanes = cell.shape
    n, ntx, nty = lax.axis_size("probe"), lax.axis_size("tx"), lax.axis_size("ty")
    field = pltpu.VMEM((np_ * (nx + 4), ny + 2 * LEAD, nz), f32)
    vmem = pl.BlockSpec(memory_space=pltpu.VMEM)
    hbm = pl.BlockSpec(memory_space=pltpu.HBM)
    return pl.pallas_call(
        functools.partial(kernel, np_, nx, ny),
        out_shape=(
            jax.ShapeDtypeStruct((1, lanes // nty), f32),
            jax.ShapeDtypeStruct((1, 1), jnp.int32),
            jax.ShapeDtypeStruct((nx, ny, np_ * nz), f32),
        ),
        in_specs=[hbm, hbm, vmem, vmem, vmem, vmem],
        out_specs=(vmem, pl.BlockSpec(memory_space=pltpu.SMEM), hbm),
        scratch_shapes=[
            field,
            field,
            pltpu.VMEM((7, nx + 2, ny, nz), f32),
            pltpu.VMEM((2, 7, nx, nz), f32),
            pltpu.VMEM((2, 7, nx, nz), f32),
            pltpu.VMEM((2, 2, np_, 2, ny, nz), f32),
            pltpu.VMEM((2, 2, np_, 2, nx, nz), f32),
            pltpu.VMEM((2, 4, np_, 1, nz), f32),
            pltpu.VMEM((2, np_, 2, nx, nz), f32),
            pltpu.VMEM((4, np_, 1, nz), f32),
            pltpu.VMEM((16 * lines, lanes), f32),
            pltpu.VMEM((CAPACITY, 16), f32),
            pltpu.VMEM((lines, 1, lanes), f32),
            pltpu.VMEM((n * ntx * nty, 1, lanes), f32),
            pltpu.SemaphoreType.DMA((np_,)),
            pltpu.SemaphoreType.DMA((7,)),
            pltpu.SemaphoreType.DMA((8, np_)),
            pltpu.SemaphoreType.DMA((2, 8, np_)),
            pltpu.SemaphoreType.DMA((4,)),
            pltpu.SemaphoreType.DMA((4,)),
            pltpu.SemaphoreType.DMA,
            pltpu.SemaphoreType.DMA,
        ],
        compiler_params=pltpu.CompilerParams(collective_id=0, has_side_effects=True, vmem_limit_bytes=56 << 20),
        name="stencil",
    )(probes, coupling, cell, frac, noise, slot)


def sensors_of_any_number(field, cell, frac, noise, slot, np_, nx, ny, total_y):
    cell, frac, noise, slot = (a.reshape(-1) for a in (cell, frac, noise, slot))
    local_x = cell // (total_y * 128) - lax.axis_index("tx") * nx
    local_y = cell // 128 % total_y - lax.axis_index("ty") * ny
    height = cell % 128
    inside = (local_x >= 0) & (local_x < nx) & (local_y >= 0) & (local_y < ny)
    line = jnp.clip(local_x, 0, nx - 1) * ny + jnp.clip(local_y, 0, ny - 1)
    picked = jnp.take(field, line, axis=0).reshape(-1, np_, 128)
    heights = jnp.arange(128, dtype=jnp.int32)[None, :]
    below = jnp.sum(jnp.where((heights == height[:, None])[:, None], picked, 0.0), axis=2)
    above = jnp.sum(jnp.where((heights == height[:, None] + 1)[:, None], picked, 0.0), axis=2)
    values = (1.0 - frac)[:, None] * below + frac[:, None] * above
    terms = jnp.where(inside, -jnp.sum(values * values, axis=1) / noise, 0.0)
    ordered = jnp.zeros_like(terms).at[slot].set(terms)
    return lax.psum_scatter(ordered, ("probe", "tx", "ty"), scatter_dimension=0, tiled=True)


def shards(probes, coupling, sensor_cell, sensor_frac, noise_var, owner_slot):
    np_, nx, ny, nz = probes.shape
    small = [a.reshape(-1, 128) for a in (sensor_cell, sensor_frac, noise_var, owner_slot)]
    gradient, crowded, field = whole(probes, coupling, *small)
    sizes = (np_, nx, ny, ny * lax.axis_size("ty"))
    return lax.cond(
        crowded[0, 0] > 0,
        lambda: sensors_of_any_number(field.reshape(nx * ny, np_ * nz), *small, *sizes),
        lambda: gradient.reshape(-1),
    )


def solution(mesh):
    in_specs = (P("probe", "tx", "ty", None), P(None, "tx", "ty", None), P(), P(), P(), P())
    out_specs = P(("probe", "tx", "ty"))
    return jax.shard_map(shards, mesh=mesh, in_specs=in_specs, out_specs=out_specs, check_vma=False)
```

time: 62.3 us -> 58.2 us (0.934)
  Pallas kernels: 60.9 us -> 56.8 us
    pallas_call x2 -> x1, Pallas kernels: 60.9 us -> 56.8 us  [whole(): pl.pallas_call(functools.partial(kernel, np_, nx, ny), out_shape=(jax.Sha...]
where the time goes in v5:
time: 58.2 us; the launch traced here: 58.1 us
  Pallas kernels  56.8 us (98%)
  between operations  0.75 us (1%)
    pallas_call x1, Pallas kernels, whole(): pl.pallas_call(functools.partial(kernel, np_, nx, ny), out_shape=(jax.Sha...  56.8 us

profile of v5, /device:TPU:1, one launch (start us, length us, event | category | flops | bytes accessed | tf_op | source)
XLA Modules:
  0.0 58.1 jit_solution(1118151782246494620)
XLA Ops:
  0.0 0.0 copy-start
  0.0 0.0 copy-start.1
  0.0 0.0 copy-start.2
  0.0 0.0 copy-start.3
  0.0 56.8 %stencil.1 = (f32[1,32]{1,0:T(1,128)S(1)}, s32[1,1]{1,0:T(1,128)}, f32[32,32,512]{2,1,0:T(8,128)S(1)}) custom-call(f32[4,32,32,128]{3,2,1,0:T(8,128)} %probes_hbm.1, f32[7,32,32,128]{3,2,1,0:T(8,128)} %coup_hbm.1, s32[32,128]{1,0:T(8,128)} %bitcast.8, f32[32,128]{1,0:T(8,128)} %bitcast.9, f32[32,128]{1,0:T(8,128)} %bitcast.11, s32[32,128]{1,0:T(8,128)} %bitcast.10), custom_call_target="tpu_custom_call" | custom-call | tf_op jit(solution)/shard_map/stencil/pallas_call | solution.py:426
  57.5 0.0 copy-done
  57.5 0.0 copy-done.1
  57.5 0.0 copy-done.2
  57.5 0.0 copy-done.3
  57.6 0.5 copy.19
  (1 shorter events, 0.0 us)
Async XLA Ops:
  0.0 57.5 %copy-start = (s32[4096]{0:T(1024)S(1)}, s32[4096]{0:T(1024)}, u32[]{:S(2)}) copy-start(s32[4096]{0:T(1024)} %param.10) | copy-start | bytes 49156
  0.0 57.5 %copy-start.1 = (f32[4096]{0:T(1024)S(1)}, f32[4096]{0:T(1024)}, u32[]{:S(2)}) copy-start(f32[4096]{0:T(1024)} %param.11) | copy-start | bytes 49156
  0.0 57.5 %copy-start.2 = (s32[4096]{0:T(1024)S(1)}, s32[4096]{0:T(1024)}, u32[]{:S(2)}) copy-start(s32[4096]{0:T(1024)} %param.13) | copy-start | bytes 49156
  0.0 57.5 %copy-start.3 = (f32[4096]{0:T(1024)S(1)}, f32[4096]{0:T(1024)}, u32[]{:S(2)}) copy-start(f32[4096]{0:T(1024)} %param.12) | copy-start | bytes 49156

commit v6 on v5

--- a/solution.py
+++ b/solution.py
@@ -19,8 +19,8 @@
 
 def kernel(
     np_, nx, ny, probes_hbm, coup_hbm, cell, frac, noise, slot,
-    out, crowded, out_hbm,
-    va, vb, c, cyrecv, cysend, xrecv, yrecv, krecv, ysend, ksend, data, chosen, terms, gathered,
+    out, crowded,
+    va, vb, c, cyrecv, cysend, xrecv, yrecv, krecv, ysend, ksend, data, chosen, hot, weight, energy, terms, gathered,
     load_sem, coup_sem, send_sem, recv_sem, csend_sem, crecv_sem, sum_send, sum_recv,
 ):
     planes = nx + 4
@@ -87,7 +87,6 @@
         for q in (0, 1, nx + 2, nx + 3):
             for t in range(ny // 8):
                 va[p * planes + q, pl.ds(LEAD + 8 * t, 8)] = tile
-    choose_sensors(nx, ny, nty, ntx, tx, ty, cell, frac, noise, slot, crowded, data, chosen)
     pl.semaphore_wait(barrier, n_probe - 1 + sum(h.astype(jnp.int32) for h in to))
 
     def copy(d, par, p):
@@ -196,6 +195,7 @@
 
     for p in range(1, np_):
         first_send(p)
+    choose_sensors(nx, ny, nty, ntx, tx, ty, cell, frac, noise, slot, crowded, data, chosen, hot, weight, energy)
     for d in (0, 1, 2, 3):
 
         @pl.when(from_[d])
@@ -240,18 +240,17 @@
                 up, down = (outer, inner) if side == 0 else (inner, outer)
                 fb[along_x(p, 8 * t, y, 8), :] = combine(coef, v, ahead, behind, up, down)
 
-    def save(p):
-        return pltpu.make_async_copy(
-            va.at[pl.ds(p * planes + 2, nx), pl.ds(LEAD, ny)], out_hbm.at[:, :, pl.ds(p * 128, 128)], load_sem.at[p]
-        )
-
-    def work(n, _):
-        block, p = n // np_, lax.rem(n, np_)
+    def work(block, _):
+        for p in range(np_):
+            work_on(block, p)
+        return 0
+
+    def work_on(block, p):
         par = lax.rem(block, 2)
         receive(par, p)
+        wait_sent(p)
         sweep(va, vb, p, -1, nx + 2, (0, 1, 2, 3))
         outer_rows(par, p)
-        wait_sent(p)
         sweep(vb, va, p, 0, nx, (0, 3))
 
         @pl.when(block < blocks - 1)
@@ -267,13 +266,11 @@
 
         @pl.when(block == blocks - 1)
         def _():
-            save(p).start()
-
-        return 0
-
-    lax.fori_loop(0, blocks * np_, work, 0)
-
-    sensor_terms(np_, nx, ny, planes, va, chosen, terms)
+            add_energy(nx, ny, p * planes + 2, va, hot, weight, energy)
+
+    lax.fori_loop(0, blocks, work, 0)
+
+    sensor_terms(chosen, energy, terms)
     offsets = [(k, a, b) for k in range(n_probe) for a in range(ntx) for b in range(nty)]
     place = {o: i for i, o in enumerate(offsets)}
 
@@ -299,8 +296,6 @@
         def _(d=d):
             copy_coupling(d).wait_send()
 
-    for p in range(np_):
-        save(p).wait()
     others = gathered.at[pl.ds(1, len(offsets) - 1)]
     every = pltpu.make_async_remote_copy(
         src_ref=others,
@@ -341,7 +336,7 @@
     return lax.broadcasted_iota(jnp.int32, shape, dim)
 
 
-def choose_sensors(nx, ny, nty, ntx, tx, ty, cell, frac, noise, slot, crowded, data, chosen):
+def choose_sensors(nx, ny, nty, ntx, tx, ty, cell, frac, noise, slot, crowded, data, chosen, hot, weight, energy):
     lines, lanes = cell.shape
     bf16, f32 = jnp.bfloat16, jnp.float32
     total_y = ny * nty
@@ -377,39 +372,40 @@
     row_id = iota((CAPACITY, lanes), 0)
     picked = jnp.zeros((CAPACITY, 16), f32)
     for r in range(lines):
-        hot = jnp.where(rank[r : r + 1, :] == row_id, 1.0, 0.0).astype(bf16)
-        picked = picked + dot(hot, data[pl.ds(16 * r, 16), :].astype(bf16), ((1,), (1,)))
+        one = jnp.where(rank[r : r + 1, :] == row_id, 1.0, 0.0).astype(bf16)
+        picked = picked + dot(one, data[pl.ds(16 * r, 16), :].astype(bf16), ((1,), (1,)))
     chosen[...] = picked
-
-
-def sensor_terms(np_, nx, ny, planes, field, chosen, terms):
-    bf16, f32 = jnp.bfloat16, jnp.float32
+    line = (picked[:, 0:1] * ny + picked[:, 1:2]).astype(jnp.int32)
+    lane_id = iota((CAPACITY, lanes), 1)
+    for b in range(nx * ny // lanes):
+        hot[:, b * lanes : (b + 1) * lanes] = jnp.where(line - b * lanes == lane_id, 1.0, 0.0).astype(bf16)
+    height = picked[:, 2:3].astype(jnp.int32)
+    above = picked[:, 6:7] + picked[:, 7:8] + picked[:, 8:9]
+    weight[...] = jnp.where(lane_id == height, 1.0 - above, 0.0) + jnp.where(lane_id == height + 1, above, 0.0)
+    energy[...] = jnp.zeros_like(energy)
+
+
+def add_energy(nx, ny, first, field, hot, weight, energy):
+    lanes = field.shape[2]
+    deep = 2 * lanes
+    count = deep // ny
+    got = jnp.zeros((CAPACITY, lanes), jnp.float32)
+    for b in range(nx * ny // deep):
+        cells = field[pl.ds(first + b * count, count), pl.ds(LEAD, ny)].reshape(deep, lanes)
+        for piece in split(cells, 2):
+            got = got + dot(hot[:, b * deep : (b + 1) * deep], piece)
+    value = jnp.sum(got * weight[...], axis=1, keepdims=True)
+    energy[...] += value * value
+
+
+def sensor_terms(chosen, energy, terms):
     lines, _, lanes = terms.shape
-    lane_id = iota((CAPACITY, lanes), 1)
     picked = chosen[...]
-    local_x, local_y, height, valid, line, lane = (picked[:, k : k + 1].astype(jnp.int32) for k in range(6))
-    above = picked[:, 6:7] + picked[:, 7:8] + picked[:, 8:9]
+    valid, line, lane = (picked[:, k : k + 1].astype(jnp.int32) for k in (3, 4, 5))
     variance = picked[:, 9:10] + picked[:, 10:11] + picked[:, 11:12]
-    got = jnp.zeros((CAPACITY, np_ * lanes), f32)
-    at = local_x * ny + local_y
-    deep = 2 * lanes
-    wide_id = iota((CAPACITY, deep), 1)
-    for b in range(nx * ny // deep):
-        hot = jnp.where(at - b * deep == wide_id, 1.0, 0.0).astype(bf16)
-        count = deep // ny
-        cells = [
-            field[pl.ds(p * planes + 2 + b * count, count), pl.ds(LEAD, ny)].reshape(deep, lanes) for p in range(np_)
-        ]
-        for piece in split(jnp.concatenate(cells, axis=1), 2):
-            got = got + dot(hot, piece)
-    weight = jnp.where(lane_id == height, 1.0 - above, 0.0) + jnp.where(lane_id == height + 1, above, 0.0)
-    energy = jnp.zeros((CAPACITY, 1), f32)
-    for p in range(np_):
-        value = jnp.sum(got[:, p * lanes : (p + 1) * lanes] * weight, axis=1, keepdims=True)
-        energy = energy + value * value
-    grad = jnp.where(valid > 0, -energy / jnp.where(valid > 0, variance, 1.0), 0.0)
+    grad = jnp.where(valid > 0, -energy[...] / jnp.where(valid > 0, variance, 1.0), 0.0)
     to_line = jnp.where(iota((CAPACITY, lines), 1) == line, 1.0, 0.0)
-    to_lane = jnp.where(lane_id == lane, grad, 0.0)
+    to_lane = jnp.where(iota((CAPACITY, lanes), 1) == lane, grad, 0.0)
     ordered = dot(to_line, to_lane, ((0,), (0,)), precision=lax.Precision.HIGHEST)
     for n in range(lines):
         terms[n] = ordered[n : n + 1, :]
@@ -428,10 +424,9 @@
         out_shape=(
             jax.ShapeDtypeStruct((1, lanes // nty), f32),
             jax.ShapeDtypeStruct((1, 1), jnp.int32),
-            jax.ShapeDtypeStruct((nx, ny, np_ * nz), f32),
         ),
         in_specs=[hbm, hbm, vmem, vmem, vmem, vmem],
-        out_specs=(vmem, pl.BlockSpec(memory_space=pltpu.SMEM), hbm),
+        out_specs=(vmem, pl.BlockSpec(memory_space=pltpu.SMEM)),
         scratch_shapes=[
             field,
             field,
@@ -445,6 +440,9 @@
             pltpu.VMEM((4, np_, 1, nz), f32),
             pltpu.VMEM((16 * lines, lanes), f32),
             pltpu.VMEM((CAPACITY, 16), f32),
+            pltpu.VMEM((CAPACITY, nx * ny), jnp.bfloat16),
+            pltpu.VMEM((CAPACITY, lanes), f32),
+            pltpu.VMEM((CAPACITY, 1), f32),
             pltpu.VMEM((lines, 1, lanes), f32),
             pltpu.VMEM((n * ntx * nty, 1, lanes), f32),
             pltpu.SemaphoreType.DMA((np_,)),
@@ -456,38 +454,56 @@
             pltpu.SemaphoreType.DMA,
             pltpu.SemaphoreType.DMA,
         ],
-        compiler_params=pltpu.CompilerParams(collective_id=0, has_side_effects=True, vmem_limit_bytes=56 << 20),
+        compiler_params=pltpu.CompilerParams(collective_id=0, has_side_effects=True, vmem_limit_bytes=67_000_000),
         name="stencil",
     )(probes, coupling, cell, frac, noise, slot)
 
 
-def sensors_of_any_number(field, cell, frac, noise, slot, np_, nx, ny, total_y):
-    cell, frac, noise, slot = (a.reshape(-1) for a in (cell, frac, noise, slot))
-    local_x = cell // (total_y * 128) - lax.axis_index("tx") * nx
-    local_y = cell // 128 % total_y - lax.axis_index("ty") * ny
-    height = cell % 128
+def general(probes, coupling, cell, frac, noise, slot):
+    np_, nx, ny, nz = probes.shape
+
+    def neighbour(block, axis, dim, step):
+        count = lax.axis_size(axis)
+        size = block.shape[dim]
+        edge = lax.slice_in_dim(block, 0, 1, axis=dim) if step > 0 else lax.slice_in_dim(block, size - 1, size, axis=dim)
+        edge = lax.ppermute(edge, axis, [(i, i - step) for i in range(count) if 0 <= i - step < count])
+        if step > 0:
+            return jnp.concatenate([lax.slice_in_dim(block, 1, None, axis=dim), edge], axis=dim)
+        return jnp.concatenate([edge, lax.slice_in_dim(block, 0, size - 1, axis=dim)], axis=dim)
+
+    def advance(_, v):
+        deep = jnp.pad(v, ((0, 0), (0, 0), (0, 0), (1, 1)))
+        r = coupling[0] * v
+        r = r + coupling[1] * neighbour(v, "tx", 1, 1) + coupling[2] * neighbour(v, "tx", 1, -1)
+        r = r + coupling[3] * neighbour(v, "ty", 2, 1) + coupling[4] * neighbour(v, "ty", 2, -1)
+        return r + coupling[5] * deep[..., 2:] + coupling[6] * deep[..., :-2]
+
+    field = lax.fori_loop(1, STEPS, advance, advance(0, probes)).reshape(np_, nx * ny, nz)
+    total_y = ny * lax.axis_size("ty")
+    local_x = cell // (total_y * nz) - lax.axis_index("tx") * nx
+    local_y = cell // nz % total_y - lax.axis_index("ty") * ny
+    height = (cell % nz)[:, None]
     inside = (local_x >= 0) & (local_x < nx) & (local_y >= 0) & (local_y < ny)
     line = jnp.clip(local_x, 0, nx - 1) * ny + jnp.clip(local_y, 0, ny - 1)
-    picked = jnp.take(field, line, axis=0).reshape(-1, np_, 128)
-    heights = jnp.arange(128, dtype=jnp.int32)[None, :]
-    below = jnp.sum(jnp.where((heights == height[:, None])[:, None], picked, 0.0), axis=2)
-    above = jnp.sum(jnp.where((heights == height[:, None] + 1)[:, None], picked, 0.0), axis=2)
-    values = (1.0 - frac)[:, None] * below + frac[:, None] * above
-    terms = jnp.where(inside, -jnp.sum(values * values, axis=1) / noise, 0.0)
+    heights = jnp.arange(nz, dtype=jnp.int32)[None, :]
+
+    def energy(p, total):
+        picked = jnp.take(field[p], line, axis=0)
+        below = jnp.sum(jnp.where(heights == height, picked, 0.0), axis=1)
+        above = jnp.sum(jnp.where(heights == height + 1, picked, 0.0), axis=1)
+        value = (1.0 - frac) * below + frac * above
+        return total + value * value
+
+    energies = lax.fori_loop(0, np_, energy, jnp.zeros_like(frac))
+    terms = jnp.where(inside, -energies / noise, 0.0)
     ordered = jnp.zeros_like(terms).at[slot].set(terms)
     return lax.psum_scatter(ordered, ("probe", "tx", "ty"), scatter_dimension=0, tiled=True)
 
 
 def shards(probes, coupling, sensor_cell, sensor_frac, noise_var, owner_slot):
-    np_, nx, ny, nz = probes.shape
-    small = [a.reshape(-1, 128) for a in (sensor_cell, sensor_frac, noise_var, owner_slot)]
-    gradient, crowded, field = whole(probes, coupling, *small)
-    sizes = (np_, nx, ny, ny * lax.axis_size("ty"))
-    return lax.cond(
-        crowded[0, 0] > 0,
-        lambda: sensors_of_any_number(field.reshape(nx * ny, np_ * nz), *small, *sizes),
-        lambda: gradient.reshape(-1),
-    )
+    numbers = (sensor_cell, sensor_frac, noise_var, owner_slot)
+    gradient, crowded = whole(probes, coupling, *(a.reshape(-1, 128) for a in numbers))
+    return lax.cond(crowded[0, 0] > 0, lambda: general(probes, coupling, *numbers), lambda: gradient.reshape(-1))
 
 
 def solution(mesh):

time: 58.2 us -> 56.6 us (0.973)
  Pallas kernels: 56.8 us -> 55 us
    pallas_call x1, Pallas kernels: 56.8 us -> 55 us  [whole(): pl.pallas_call(functools.partial(kernel, np_, nx, ny), out_shape=(jax.Sha...]
where the time goes in v6:
time: 56.6 us; the launch traced here: 56.4 us
  Pallas kernels  55 us (97%)
  between operations  0.66 us (1%)
    pallas_call x1, Pallas kernels, whole(): pl.pallas_call(functools.partial(kernel, np_, nx, ny), out_shape=(jax.Sha...  55 us

profile of v6, /device:TPU:1, one launch (start us, length us, event | category | flops | bytes accessed | tf_op | source)
XLA Modules:
  0.0 56.4 jit_solution(7052549476773267647)
XLA Ops:
  0.0 0.0 copy-start.3
  0.0 0.0 copy-start.4
  0.0 55.0 %stencil.1 = (f32[1,32]{1,0:T(1,128)S(1)}, s32[1,1]{1,0:T(1,128)}) custom-call(f32[4,32,32,128]{3,2,1,0:T(8,128)} %probes_hbm.1, f32[7,32,32,128]{3,2,1,0:T(8,128)} %coup_hbm.1, s32[32,128]{1,0:T(8,128)} %bitcast.58, f32[32,128]{1,0:T(8,128)} %bitcast.57, f32[32,128]{1,0:T(8,128)} %bitcast.59, s32[32,128]{1,0:T(8,128)} %bitcast.60), custom_call_target="tpu_custom_call" | custom-call | tf_op jit(solution)/shard_map/stencil/pallas_call | solution.py:422
  55.7 0.0 copy-done.3
  55.7 0.0 copy-done.4
  55.7 0.2 conditional.1
  55.9 0.5 copy.26
Async XLA Ops:
  0.0 55.7 %copy-start.3 = (f32[4096]{0:T(1024)S(1)}, f32[4096]{0:T(1024)}, u32[]{:S(2)}) copy-start(f32[4096]{0:T(1024)} %param.15) | copy-start | bytes 49156
  0.0 55.7 %copy-start.4 = (s32[4096]{0:T(1024)S(1)}, s32[4096]{0:T(1024)}, u32[]{:S(2)}) copy-start(s32[4096]{0:T(1024)} %param.14) | copy-start | bytes 49156

commit v7 on v6

--- a/solution.py
+++ b/solution.py
@@ -43,29 +43,8 @@
             probes_hbm.at[p], va.at[pl.ds(p * planes + 2, nx), pl.ds(LEAD, ny)], load_sem.at[p]
         )
 
-    def load_coupling(k):
-        return pltpu.make_async_copy(coup_hbm.at[k], c.at[k, pl.ds(1, nx)], coup_sem.at[k])
-
-    load(0).start()
-    for k in range(7):
-        load_coupling(k).start()
-    for p in range(1, np_):
-        load(p).start()
-
-    tile = jnp.zeros((8, 128), jnp.float32)
-
-    for k in range(7):
-        for t in range(ny // 8):
-            for q in (0, nx + 1):
-                c[k, q, pl.ds(8 * t, 8)] = tile
-        for side in range(2):
-            for t in range(nx // 8):
-                cyrecv[side, k, pl.ds(8 * t, 8)] = tile
-    for par in range(2):
-        for side in range(2):
-            for p in range(np_):
-                for t in range(nx // 8):
-                    yrecv[par, side, p, 1, pl.ds(8 * t, 8)] = tile
+    def all_coupling():
+        return pltpu.make_async_copy(coup_hbm, c.at[:, pl.ds(1, nx)], coup_sem)
 
     barrier = pltpu.get_barrier_semaphore()
     for d in range(8):
@@ -76,6 +55,31 @@
 
     for k in range(1, n_probe):
         pl.semaphore_signal(barrier, inc=1, device_id={"probe": lax.rem(me + k, n_probe)}, device_id_type=MESH)
+
+    load(0).start()
+    all_coupling().start()
+    for p in range(1, np_):
+        load(p).start()
+
+    tile = jnp.zeros((8, 128), jnp.float32)
+    for d in X_DIRS:
+
+        @pl.when(jnp.logical_not(from_[d]))
+        def _(d=d):
+            for k in range(7):
+                for t in range(ny // 8):
+                    c[k, nx + 1 if d == 0 else 0, pl.ds(8 * t, 8)] = tile
+
+    for d in Y_DIRS:
+
+        @pl.when(jnp.logical_not(from_[d]))
+        def _(d=d):
+            for t in range(nx // 8):
+                for k in range(7):
+                    cyrecv[d - 2, k, pl.ds(8 * t, 8)] = tile
+                for par in range(2):
+                    for p in range(np_):
+                        yrecv[par, d - 2, p, 1, pl.ds(8 * t, 8)] = tile
 
     def zero_field(q, _):
         va[q, pl.ds(0, 8)] = tile
@@ -133,17 +137,19 @@
             def _(d=d):
                 copy(d, par, p).start()
 
-    def pack_y(p):
+    def send_y(par, p):
         for side, edge in enumerate(((0, 1), (ny - 1, ny - 2))):
             for n, y in enumerate(edge):
                 ysend[side, p, n] = fa[along_x(p, 0, y, nx), :]
+            start((2 + side,), par, p)
         for d in CORNERS:
             sx, sy = DIRECTIONS[d]
             x, y = (0 if sx < 0 else nx - 1), (0 if sy < 0 else ny - 1)
             ksend[d - 4, p] = va[p * planes + x + 2, pl.ds(LEAD + y, 1)]
-
-    def receive(par, p):
-        for d in (0, 1, 4, 5, 6, 7, 2, 3):
+        start(CORNERS, par, p)
+
+    def receive(dirs, par, p):
+        for d in dirs:
 
             @pl.when(from_[d])
             def _(d=d):
@@ -168,12 +174,11 @@
 
     def first_send(p):
         load(p).wait()
-        pack_y(p)
-        start((2, 3, 4, 5, 6, 7, 0, 1), 0, p)
+        send_y(0, p)
+        start(X_DIRS, 0, p)
 
     first_send(0)
-    for k in range(7):
-        load_coupling(k).wait()
+    all_coupling().wait()
     lane = lax.broadcasted_iota(jnp.int32, (8, 128), 1)
 
     def clip_edges(i, _):
@@ -247,22 +252,21 @@
 
     def work_on(block, p):
         par = lax.rem(block, 2)
-        receive(par, p)
         wait_sent(p)
+        receive((0, 1, 4, 5, 6, 7, 2, 3), par, p)
         sweep(va, vb, p, -1, nx + 2, (0, 1, 2, 3))
         outer_rows(par, p)
         sweep(vb, va, p, 0, nx, (0, 3))
 
         @pl.when(block < blocks - 1)
         def _():
-            pack_y(p)
-            start((2, 3, 4, 5, 6, 7), 1 - par, p)
+            send_y(1 - par, p)
 
         sweep(vb, va, p, 0, nx, (1, 2))
 
         @pl.when(block < blocks - 1)
         def _():
-            start((0, 1), 1 - par, p)
+            start(X_DIRS, 1 - par, p)
 
         @pl.when(block == blocks - 1)
         def _():
@@ -446,7 +450,7 @@
             pltpu.VMEM((lines, 1, lanes), f32),
             pltpu.VMEM((n * ntx * nty, 1, lanes), f32),
             pltpu.SemaphoreType.DMA((np_,)),
-            pltpu.SemaphoreType.DMA((7,)),
+            pltpu.SemaphoreType.DMA,
             pltpu.SemaphoreType.DMA((8, np_)),
             pltpu.SemaphoreType.DMA((2, 8, np_)),
             pltpu.SemaphoreType.DMA((4,)),

time: 56.6 us -> 56.4 us (level)
  no operation moved by 1% of the time
where the time goes in v7:
time: 56.4 us; the launch traced here: 56.2 us
  Pallas kernels  54.8 us (97%)
  between operations  0.66 us (1%)
    pallas_call x1, Pallas kernels, whole(): pl.pallas_call(functools.partial(kernel, np_, nx, ny), out_shape=(jax.Sha...  54.8 us

profile of v7, /device:TPU:1, one launch (start us, length us, event | category | flops | bytes accessed | tf_op | source)
XLA Modules:
  0.0 56.2 jit_solution(11279221206126739581)
XLA Ops:
  0.0 0.0 copy-start.3
  0.0 0.0 copy-start.4
  0.0 54.8 %stencil.1 = (f32[1,32]{1,0:T(1,128)S(1)}, s32[1,1]{1,0:T(1,128)}) custom-call(f32[4,32,32,128]{3,2,1,0:T(8,128)} %probes_hbm.1, f32[7,32,32,128]{3,2,1,0:T(8,128)} %coup_hbm.1, s32[32,128]{1,0:T(8,128)} %bitcast.58, f32[32,128]{1,0:T(8,128)} %bitcast.57, f32[32,128]{1,0:T(8,128)} %bitcast.59, s32[32,128]{1,0:T(8,128)} %bitcast.60), custom_call_target="tpu_custom_call" | custom-call | tf_op jit(solution)/shard_map/stencil/pallas_call | solution.py:426
  55.4 0.0 copy-done.3
  55.4 0.0 copy-done.4
  55.5 0.2 conditional.1
  55.7 0.5 copy.26
Async XLA Ops:
  0.0 55.4 %copy-start.3 = (f32[4096]{0:T(1024)S(1)}, f32[4096]{0:T(1024)}, u32[]{:S(2)}) copy-start(f32[4096]{0:T(1024)} %param.15) | copy-start | bytes 49156
  0.0 55.4 %copy-start.4 = (s32[4096]{0:T(1024)S(1)}, s32[4096]{0:T(1024)}, u32[]{:S(2)}) copy-start(s32[4096]{0:T(1024)} %param.14) | copy-start | bytes 49156
